TPU v7x, 768 devices: a whole 4x8x12 slice. The times are simulated.
768 devices in a mesh: lat: 24 (over z, core), lon: 32 (over x, y).
Axes of the slice: x: 4, y: 8, z: 12, core: 2. Of those that a mesh axis runs over, the one named last changes fastest.
Arguments:
- ensemble: float32 [768, 4096, 128], P('lat', 'lon'), may hold values from -6 to 6
- observed: float32 [2, 24, 32, 8], P(None, 'lat', 'lon'), may hold values from -8 to 8
- precision: float32 [2, 24, 32, 8], P(None, 'lat', 'lon'), may hold values from 0.05 to 0.5
- interp_weight: float32 [2, 24, 32, 4, 8], P(None, 'lat', 'lon'), may hold values from 0.1 to 1
- stencil: int32 [2, 24, 32, 4, 8], P(None, 'lat', 'lon'), may hold values from 0 to 4419, as said below
- owned: int32 [2, 24, 32, 8], P(None, 'lat', 'lon'), may hold values from 0 to 1, as said below
- pattern: int32 [2, 24, 32, 5, 32], P(None, 'lat', 'lon'), may hold values 0 or 1
Outputs:
- analysis: float32 [768, 4096, 128], P('lat', 'lon')
Inputs may be any that keep to these rules, and one draw needn't show every extreme that they name: `stencil`: each index names one of the four corners of a 2 x 2 square of cells of the rim-extended tile, in the order (0,0), (0,1), (1,0), (1,1). In each batch and tile the owned slots come first and there is at least one; some tile owns all 8 slots in every batch.
All inputs are finite; a program needn't handle non-finite values. No bound on the sum of `pattern` on one device may be relied on, other than what follows from the above.
Results may differ from a plain program's by a relative error of at most 0.0026.
Values may be sent and summed in bfloat16 or wider, within the bound.
A program may use at most 32 MiB of HBM per device.

v0:
```python
import jax
import jax.numpy as jnp
from jax import lax
from jax.sharding import PartitionSpec as P

BATCHES = 2
REACH = 2


def with_halo(array, sides, width):
    for axis, dim in sides:
        peers, length = (lax.axis_size(axis), array.shape[dim])
        up = [(i, (i + 1) % peers) for i in range(peers)]
        down = [(j, i) for i, j in up]
        last = lax.slice_in_dim(array, length - width, length, axis=dim)
        first = lax.slice_in_dim(array, 0, width, axis=dim)
        before = lax.ppermute(last, axis, up)
        after = lax.ppermute(first, axis, down)
        array = jnp.concatenate([before, array, after], axis=dim)
    return array


def shifted(block, axis, distance):
    devices = range(lax.axis_size(axis))
    route = [(i - distance, i) for i in devices if i - distance in devices]
    return lax.ppermute(block, axis, route)


def square_root(gram, proj):
    members = gram.shape[-1]
    eye = jnp.eye(members, dtype=jnp.float32)
    system = gram + (members - 1.0) * eye
    factor = jnp.linalg.cholesky(system)
    lower_sol = jax.scipy.linalg.solve_triangular(factor, proj[..., None], lower=True)
    weights = jax.scipy.linalg.solve_triangular(factor, lower_sol, lower=True, trans=1)
    inverse = jax.scipy.linalg.solve_triangular(factor, eye, lower=True)
    return jnp.sqrt(members - 1.0) * jnp.swapaxes(inverse, -1, -2) + weights


def weighted_terms(scaled_rows, innov_rows, marks):
    members = scaled_rows.shape[-1]
    weighted = scaled_rows * marks.astype(jnp.bfloat16)[:, None, None]
    flat_weighted = weighted.reshape(-1, members)
    gram_term = jnp.dot(
        flat_weighted.T, scaled_rows.reshape(-1, members), preferred_element_type=jnp.float32
    )
    proj_term = jnp.dot(innov_rows.reshape(-1), flat_weighted, preferred_element_type=jnp.float32)
    return (gram_term, proj_term)


def local(ensemble, observed, precision, interp_weight, stencil, owned, pattern):
    members = ensemble.shape[-1]
    lat_count = lax.axis_size("lat")
    my_lat = lax.axis_index("lat")
    analysis = ensemble
    for batch_no in range(BATCHES):
        padded = with_halo(analysis, (("lat", 0), ("lon", 1)), 1)
        row_ids = jnp.arange(padded.shape[0], dtype=jnp.int32)[:, None, None]
        cut_top = (row_ids == 0) & (my_lat == 0)
        cut_bottom = (row_ids == padded.shape[0] - 1) & (my_lat == lat_count - 1)
        padded = jnp.where(cut_top | cut_bottom, 0.0, padded)
        flat_cells = padded.reshape(-1, members)
        values = flat_cells[stencil[batch_no, 0, 0]]
        prior = jnp.sum(interp_weight[batch_no, 0, 0][..., None] * values, axis=0)
        mean_prior = jnp.mean(prior, axis=-1)
        root = jnp.sqrt(precision[batch_no, 0, 0]) * owned[batch_no, 0, 0].astype(jnp.float32)
        scaled = (root[:, None] * (prior - mean_prior[:, None])).astype(jnp.bfloat16)
        innov = (root * (observed[batch_no, 0, 0] - mean_prior)).astype(jnp.bfloat16)
        marks_all = pattern[batch_no, 0, 0].astype(jnp.float32)
        gram = jnp.zeros((members, members), jnp.float32)
        proj = jnp.zeros((members,), jnp.float32)
        row_scaled, row_innov = (
            lax.all_gather(scaled[None], "lon", axis=0, tiled=True),
            lax.all_gather(innov[None], "lon", axis=0, tiled=True),
        )
        for offset in range(-REACH, REACH + 1):
            if offset == 0:
                near_scaled, near_innov = (row_scaled, row_innov)
            else:
                near_scaled, near_innov = shifted((row_scaled, row_innov), "lat", -offset)
            gram_term, proj_term = weighted_terms(
                near_scaled, near_innov, marks_all[offset + REACH]
            )
            gram = gram + gram_term
            proj = proj + proj_term
        transform = square_root(gram, proj)
        center = jnp.mean(analysis, axis=-1, keepdims=True)
        spread = (analysis - center).reshape(-1, members)
        moved = jnp.dot(
            spread, transform, precision=lax.Precision.HIGHEST, preferred_element_type=jnp.float32
        )
        analysis = center + moved.reshape(analysis.shape)
    return analysis


def solution(mesh):
    placed = (
        P("lat", "lon", None),
        P(None, "lat", "lon", None),
        P(None, "lat", "lon", None),
        P(None, "lat", "lon", None, None),
        P(None, "lat", "lon", None, None),
        P(None, "lat", "lon", None),
        P(None, "lat", "lon", None, None),
    )
    return jax.shard_map(
        local, mesh=mesh, in_specs=placed, out_specs=P("lat", "lon", None), check_vma=False
    )
```

profile of v0, /device:TPU:1, one launch (start us, length us, event | category | flops | bytes accessed | tf_op | source)
XLA Modules:
  0.0 352.9 jit_solution(13249589013435231986)
XLA Ops:
  0.9 10.5 %collective-permute-start.1 = (f32[1,128,128]{2,1,0:T(8,128)S(1)}, f32[1,128,128]{2,1,0:T(8,128)S(1)}, u32[]{:S(2)}, u32[]{:S(2)}) collective-permute-start(f32[1,128,128]{2,1,0:T(8,128)S(1)} %get-tuple-element.21), channel_id=1, source_target_pairs={{32,0},{64,32},{96,64},{128,96},{160,128},{192,160},{224,192},{256... | collective-permute-start | bytes 196616 | tf_op jit(solution)/shard_map/ppermute | solution.py:18
  20.8 6.0 %collective-permute-start.3 = (f32[34,1,128]{2,1,0:T(1,128)S(1)}, f32[34,1,128]{2,1,0:T(1,128)S(1)}, u32[]{:S(2)}, u32[]{:S(2)}) collective-permute-start(f32[34,1,128]{2,1,0:T(1,128)S(1)} %get-tuple-element.16), channel_id=1, source_target_pairs={{1,0},{2,1},{3,2},{4,3},{5,4},{6,5},{7,6},{8,7},{9,8},{10,9},{11,1... | collective-permute-start | bytes 52232 | tf_op jit(solution)/shard_map/ppermute | solution.py:18
  29.4 3.8 %broadcast_select_fusion.1 = f32[4420,128]{1,0:T(8,128)S(1)} fusion(f32[4420,128]{1,0:T(8,128)} %concatenate.18, pred[4420]{0:T(1024)(128)(4,1)S(1)} %broadcast_in_dim.26), kind=kLoop, calls=%fused_computation.11 | loop fusion | flops 565760 | bytes 4530500 | tf_op jit(solution)/shard_map/jit(_where)/select_n | solution.py:61
  34.0 27.0 %all-gather = bf16[32,1,8]{2,1,0:T(2,128)(2,1)S(1)} all-gather(bf16[1,1,8]{2,1,0:T(2,128)(2,1)S(1)} %fusion.109), channel_id=1, replica_groups=mesh['lat'=24,'lon'=32] {'lon'}, dimensions={0}, use_global_device_ids=true | all-gather | bytes 528 | tf_op jit(solution)/shard_map/all_gather | solution.py:74
  61.1 15.6 %collective-permute-start.10 = (bf16[32,8]{0,1:T(8,128)(2,1)S(1)}, bf16[32,8]{0,1:T(8,128)(2,1)S(1)}, u32[]{:S(2)}, u32[]{:S(2)}) collective-permute-start(bf16[32,8]{0,1:T(8,128)(2,1)S(1)} %bitcast.265), channel_id=1, source_target_pairs={{32,0},{64,32},{96,64},{128,96},{160,128},{192,160},{224,192},{256... | collective-permute-start | bytes 1544 | tf_op jit(solution)/shard_map/ppermute | solution.py:26
  84.1 35.8 %all_gather.12 = bf16[32,8,128]{2,1,0:T(8,128)(2,1)S(1)} all-gather(bf16[1,8,128]{2,1,0:T(8,128)(2,1)S(1)} %fusion.95), channel_id=1, replica_groups=mesh['lat'=24,'lon'=32] {'lon'}, dimensions={0}, use_global_device_ids=true | all-gather | bytes 67584 | tf_op jit(solution)/shard_map/all_gather | solution.py:73
  120.1 14.6 %collective-permute-start.5 = (bf16[32,8,128]{2,0,1:T(8,128)(2,1)S(1)}, bf16[32,8,128]{2,0,1:T(8,128)(2,1)S(1)}, u32[]{:S(2)}, u32[]{:S(2)}) collective-permute-start(bf16[32,8,128]{2,0,1:T(8,128)(2,1)S(1)} %copy.34), channel_id=1, source_target_pairs={{0,32},{32,64},{64,96},{96,128},{128,160},{160,192},{192,224},{224... | collective-permute-start | bytes 196616 | tf_op jit(solution)/shard_map/ppermute | solution.py:26
  140.3 3.8 %collective-permute-done.7 = bf16[32,8,128]{2,0,1:T(8,128)(2,1)S(1)} collective-permute-done((bf16[32,8,128]{2,0,1:T(8,128)(2,1)S(1)}, bf16[32,8,128]{2,0,1:T(8,128)(2,1)S(1)}, u32[]{:S(2)}, u32[]{:S(2)}) %collective-permute-start.7) | collective-permute-done | bytes 65568 | tf_op jit(solution)/shard_map/ppermute | solution.py:26
  144.1 6.8 %collective-permute-start.6 = (bf16[32,8,128]{2,0,1:T(8,128)(2,1)S(1)}, bf16[32,8,128]{2,0,1:T(8,128)(2,1)S(1)}, u32[]{:S(2)}, u32[]{:S(2)}) collective-permute-start(bf16[32,8,128]{2,0,1:T(8,128)(2,1)S(1)} %copy.34), channel_id=1, source_target_pairs={{32,0},{64,32},{96,64},{128,96},{160,128},{192,160},{224,192},{256... | collective-permute-start | bytes 196616 | tf_op jit(solution)/shard_map/ppermute | solution.py:26
  154.9 11.7 %cholesky.44 = f32[128,128]{1,0:T(8,128)S(1)} custom-call(f32[128,128]{1,0:T(8,128)S(1)} %fusion.67), custom_call_target="Cholesky" | custom-call | tf_op jit(solution)/shard_map/jit(cholesky)/cholesky | solution.py:33
  168.6 9.8 %custom-call.14 = f32[1,128,128]{1,2,0:T(8,128)S(1)} custom-call(f32[1,128,128]{2,1,0:T(8,128)S(1)} %fusion.58), custom_call_target="InvertDiagBlocksLowerTriangular" | custom-call | tf_op jit(solution)/shard_map/jit(_solve_triangular)/triangular_solve | solution.py:36
  179.3 4.3 %fusion.116 = (f32[32,128]{1,0:T(8,128)S(1)}, f32[32,128,128]{2,1,0:T(8,128)S(1)}) fusion(f32[128,128,1]{1,0,2:T(8,128)S(1)} %fusion.18, f32[32,128,128]{2,1,0:T(8,128)} %param.14, f32[32,128]{1,0:T(8,128)S(1)} %broadcast_multiply_fusion.1), kind=kOutput, calls=%fused_computation.192 | convolution fusion | flops 806875136 | bytes 4292608 | tf_op jit(solution)/shard_map/dot_general | solution.py:89
  189.3 6.9 %collective-permute-start.15 = (f32[34,1,128]{2,1,0:T(1,128)S(1)}, f32[34,1,128]{2,1,0:T(1,128)S(1)}, u32[]{:S(2)}, u32[]{:S(2)}) collective-permute-start(f32[34,1,128]{2,1,0:T(1,128)S(1)} %get-tuple-element.14), channel_id=1, source_target_pairs={{1,0},{2,1},{3,2},{4,3},{5,4},{6,5},{7,6},{8,7},{9,8},{10,9},{11,1... | collective-permute-start | bytes 52232 | tf_op jit(solution)/shard_map/ppermute | solution.py:18
  201.6 4.9 %broadcast_select_fusion = f32[4420,128]{1,0:T(8,128)} fusion(f32[4420,128]{1,0:T(8,128)} %concatenate.21, pred[4420]{0:T(1024)(128)(4,1)S(1)} %broadcast_in_dim.26), kind=kLoop, calls=%fused_computation.10 | loop fusion | flops 565760 | bytes 4530500 | tf_op jit(solution)/shard_map/jit(_where)/select_n | solution.py:61
  208.9 27.1 %all-gather.1 = bf16[32,1,8]{2,1,0:T(2,128)(2,1)S(1)} all-gather(bf16[1,1,8]{2,1,0:T(2,128)(2,1)S(1)} %fusion.106), channel_id=1, replica_groups=mesh['lat'=24,'lon'=32] {'lon'}, dimensions={0}, use_global_device_ids=true | all-gather | bytes 528 | tf_op jit(solution)/shard_map/all_gather | solution.py:74
  236.2 10.4 %collective-permute-start.22 = (bf16[32,8]{0,1:T(8,128)(2,1)S(1)}, bf16[32,8]{0,1:T(8,128)(2,1)S(1)}, u32[]{:S(2)}, u32[]{:S(2)}) collective-permute-start(bf16[32,8]{0,1:T(8,128)(2,1)S(1)} %bitcast.260), channel_id=1, source_target_pairs={{32,0},{64,32},{96,64},{128,96},{160,128},{192,160},{224,192},{256... | collective-permute-start | bytes 1544 | tf_op jit(solution)/shard_map/ppermute | solution.py:26
  247.9 3.7 %collective-permute-start.21 = (bf16[32,8]{0,1:T(8,128)(2,1)S(1)}, bf16[32,8]{0,1:T(8,128)(2,1)S(1)}, u32[]{:S(2)}, u32[]{:S(2)}) collective-permute-start(bf16[32,8]{0,1:T(8,128)(2,1)S(1)} %bitcast.262), channel_id=1, source_target_pairs={{0,32},{32,64},{64,96},{96,128},{128,160},{160,192},{192,224},{224... | collective-permute-start | bytes 1544 | tf_op jit(solution)/shard_map/ppermute | solution.py:26
  251.6 3.6 %collective-permute-start.20 = (bf16[32,8]{0,1:T(8,128)(2,1)S(1)}, bf16[32,8]{0,1:T(8,128)(2,1)S(1)}, u32[]{:S(2)}, u32[]{:S(2)}) collective-permute-start(bf16[32,8]{0,1:T(8,128)(2,1)S(1)} %bitcast.263), channel_id=1, source_target_pairs={{0,64},{32,96},{64,128},{96,160},{128,192},{160,224},{192,256},{22... | collective-permute-start | bytes 1544 | tf_op jit(solution)/shard_map/ppermute | solution.py:26
  255.4 34.8 %all_gather.14 = bf16[32,8,128]{2,1,0:T(8,128)(2,1)S(1)} all-gather(bf16[1,8,128]{2,1,0:T(8,128)(2,1)S(1)} %fusion.93), channel_id=1, replica_groups=mesh['lat'=24,'lon'=32] {'lon'}, dimensions={0}, use_global_device_ids=true | all-gather | bytes 67584 | tf_op jit(solution)/shard_map/all_gather | solution.py:73
  290.5 14.8 %collective-permute-start.17 = (bf16[32,8,128]{2,0,1:T(8,128)(2,1)S(1)}, bf16[32,8,128]{2,0,1:T(8,128)(2,1)S(1)}, u32[]{:S(2)}, u32[]{:S(2)}) collective-permute-start(bf16[32,8,128]{2,0,1:T(8,128)(2,1)S(1)} %copy.47), channel_id=1, source_target_pairs={{0,32},{32,64},{64,96},{96,128},{128,160},{160,192},{192,224},{224... | collective-permute-start | bytes 196616 | tf_op jit(solution)/shard_map/ppermute | solution.py:26
  311.1 3.8 %collective-permute-done.19 = bf16[32,8,128]{2,0,1:T(8,128)(2,1)S(1)} collective-permute-done((bf16[32,8,128]{2,0,1:T(8,128)(2,1)S(1)}, bf16[32,8,128]{2,0,1:T(8,128)(2,1)S(1)}, u32[]{:S(2)}, u32[]{:S(2)}) %collective-permute-start.19) | collective-permute-done | bytes 65568 | tf_op jit(solution)/shard_map/ppermute | solution.py:26
  314.9 6.7 %collective-permute-start.18 = (bf16[32,8,128]{2,0,1:T(8,128)(2,1)S(1)}, bf16[32,8,128]{2,0,1:T(8,128)(2,1)S(1)}, u32[]{:S(2)}, u32[]{:S(2)}) collective-permute-start(bf16[32,8,128]{2,0,1:T(8,128)(2,1)S(1)} %copy.47), channel_id=1, source_target_pairs={{32,0},{64,32},{96,64},{128,96},{160,128},{192,160},{224,192},{256... | collective-permute-start | bytes 196616 | tf_op jit(solution)/shard_map/ppermute | solution.py:26
  325.5 11.7 %cholesky.55 = f32[128,128]{1,0:T(8,128)S(1)} custom-call(f32[128,128]{1,0:T(8,128)S(1)} %fusion.63), custom_call_target="Cholesky" | custom-call | tf_op jit(solution)/shard_map/jit(cholesky)/cholesky | solution.py:33
  339.2 9.8 %custom-call.17 = f32[1,128,128]{1,2,0:T(8,128)S(1)} custom-call(f32[1,128,128]{2,1,0:T(8,128)S(1)} %fusion.59), custom_call_target="InvertDiagBlocksLowerTriangular" | custom-call | tf_op jit(solution)/shard_map/jit(_solve_triangular)/triangular_solve | solution.py:36
  (119 shorter events, 64.4 us)
Async XLA Ops:
  0.9 16.6 %collective-permute-start.1 = (f32[1,128,128]{2,1,0:T(8,128)S(1)}, f32[1,128,128]{2,1,0:T(8,128)S(1)}, u32[]{:S(2)}, u32[]{:S(2)}) collective-permute-start(f32[1,128,128]{2,1,0:T(8,128)S(1)} %get-tuple-element.21), channel_id=1, source_target_pairs={{32,0},{64,32},{96,64},{128,96},{160,128},{192,160},{224,192},{256... | collective-permute-start | bytes 196616 | tf_op jit(solution)/shard_map/ppermute | solution.py:18
  11.4 3.9 %collective-permute-start = (f32[1,128,128]{2,1,0:T(8,128)S(1)}, f32[1,128,128]{2,1,0:T(8,128)S(1)}, u32[]{:S(2)}, u32[]{:S(2)}) collective-permute-start(f32[1,128,128]{2,1,0:T(8,128)S(1)} %get-tuple-element.22), channel_id=1, source_target_pairs={{0,32},{32,64},{64,96},{96,128},{128,160},{160,192},{192,224},{224... | collective-permute-start | bytes 196616 | tf_op jit(solution)/shard_map/ppermute | solution.py:17
  17.5 9.2 %collective-permute-start.2 = (f32[34,1,128]{2,1,0:T(1,128)S(1)}, f32[34,1,128]{2,1,0:T(1,128)S(1)}, u32[]{:S(2)}, u32[]{:S(2)}) collective-permute-start(f32[34,1,128]{2,1,0:T(1,128)S(1)} %get-tuple-element.15), channel_id=1, source_target_pairs={{0,1},{1,2},{2,3},{3,4},{4,5},{5,6},{6,7},{7,8},{8,9},{9,10},{10,1... | collective-permute-start | bytes 52232 | tf_op jit(solution)/shard_map/ppermute | solution.py:17
  20.8 6.9 %collective-permute-start.3 = (f32[34,1,128]{2,1,0:T(1,128)S(1)}, f32[34,1,128]{2,1,0:T(1,128)S(1)}, u32[]{:S(2)}, u32[]{:S(2)}) collective-permute-start(f32[34,1,128]{2,1,0:T(1,128)S(1)} %get-tuple-element.16), channel_id=1, source_target_pairs={{1,0},{2,1},{3,2},{4,3},{5,4},{6,5},{7,6},{8,7},{9,8},{10,9},{11,1... | collective-permute-start | bytes 52232 | tf_op jit(solution)/shard_map/ppermute | solution.py:18
  61.1 117.3 %collective-permute-start.10 = (bf16[32,8]{0,1:T(8,128)(2,1)S(1)}, bf16[32,8]{0,1:T(8,128)(2,1)S(1)}, u32[]{:S(2)}, u32[]{:S(2)}) collective-permute-start(bf16[32,8]{0,1:T(8,128)(2,1)S(1)} %bitcast.265), channel_id=1, source_target_pairs={{32,0},{64,32},{96,64},{128,96},{160,128},{192,160},{224,192},{256... | collective-permute-start | bytes 1544 | tf_op jit(solution)/shard_map/ppermute | solution.py:26
  76.7 91.7 %collective-permute-start.11 = (bf16[32,8]{0,1:T(8,128)(2,1)S(1)}, bf16[32,8]{0,1:T(8,128)(2,1)S(1)}, u32[]{:S(2)}, u32[]{:S(2)}) collective-permute-start(bf16[32,8]{0,1:T(8,128)(2,1)S(1)} %bitcast.266), channel_id=1, source_target_pairs={{64,0},{96,32},{128,64},{160,96},{192,128},{224,160},{256,192},{28... | collective-permute-start | bytes 1544 | tf_op jit(solution)/shard_map/ppermute | solution.py:26
  78.0 90.0 %collective-permute-start.9 = (bf16[32,8]{0,1:T(8,128)(2,1)S(1)}, bf16[32,8]{0,1:T(8,128)(2,1)S(1)}, u32[]{:S(2)}, u32[]{:S(2)}) collective-permute-start(bf16[32,8]{0,1:T(8,128)(2,1)S(1)} %bitcast.267), channel_id=1, source_target_pairs={{0,32},{32,64},{64,96},{96,128},{128,160},{160,192},{192,224},{224... | collective-permute-start | bytes 1544 | tf_op jit(solution)/shard_map/ppermute | solution.py:26
  81.5 86.6 %collective-permute-start.8 = (bf16[32,8]{0,1:T(8,128)(2,1)S(1)}, bf16[32,8]{0,1:T(8,128)(2,1)S(1)}, u32[]{:S(2)}, u32[]{:S(2)}) collective-permute-start(bf16[32,8]{0,1:T(8,128)(2,1)S(1)} %bitcast.268), channel_id=1, source_target_pairs={{0,64},{32,96},{64,128},{96,160},{128,192},{160,224},{192,256},{22... | collective-permute-start | bytes 1544 | tf_op jit(solution)/shard_map/ppermute | solution.py:26
  120.1 15.9 %collective-permute-start.5 = (bf16[32,8,128]{2,0,1:T(8,128)(2,1)S(1)}, bf16[32,8,128]{2,0,1:T(8,128)(2,1)S(1)}, u32[]{:S(2)}, u32[]{:S(2)}) collective-permute-start(bf16[32,8,128]{2,0,1:T(8,128)(2,1)S(1)} %copy.34), channel_id=1, source_target_pairs={{0,32},{32,64},{64,96},{96,128},{128,160},{160,192},{192,224},{224... | collective-permute-start | bytes 196616 | tf_op jit(solution)/shard_map/ppermute | solution.py:26
  136.0 2.8 collective-permute-start.4
  138.8 5.3 %collective-permute-start.7 = (bf16[32,8,128]{2,0,1:T(8,128)(2,1)S(1)}, bf16[32,8,128]{2,0,1:T(8,128)(2,1)S(1)}, u32[]{:S(2)}, u32[]{:S(2)}) collective-permute-start(bf16[32,8,128]{2,0,1:T(8,128)(2,1)S(1)} %copy.34), channel_id=1, source_target_pairs={{64,0},{96,32},{128,64},{160,96},{192,128},{224,160},{256,192},{28... | collective-permute-start | bytes 196616 | tf_op jit(solution)/shard_map/ppermute | solution.py:26
  144.1 10.4 %collective-permute-start.6 = (bf16[32,8,128]{2,0,1:T(8,128)(2,1)S(1)}, bf16[32,8,128]{2,0,1:T(8,128)(2,1)S(1)}, u32[]{:S(2)}, u32[]{:S(2)}) collective-permute-start(bf16[32,8,128]{2,0,1:T(8,128)(2,1)S(1)} %copy.34), channel_id=1, source_target_pairs={{32,0},{64,32},{96,64},{128,96},{160,128},{192,160},{224,192},{256... | collective-permute-start | bytes 196616 | tf_op jit(solution)/shard_map/ppermute | solution.py:26
  183.6 1.4 collective-permute-start.12
  183.7 3.7 %collective-permute-start.13 = (f32[1,128,128]{2,1,0:T(8,128)S(1)}, f32[1,128,128]{2,1,0:T(8,128)S(1)}, u32[]{:S(2)}, u32[]{:S(2)}) collective-permute-start(f32[1,128,128]{2,1,0:T(8,128)S(1)} %get-tuple-element.18), channel_id=1, source_target_pairs={{32,0},{64,32},{96,64},{128,96},{160,128},{192,160},{224,192},{256... | collective-permute-start | bytes 196616 | tf_op jit(solution)/shard_map/ppermute | solution.py:18
  187.4 8.8 %collective-permute-start.14 = (f32[34,1,128]{2,1,0:T(1,128)S(1)}, f32[34,1,128]{2,1,0:T(1,128)S(1)}, u32[]{:S(2)}, u32[]{:S(2)}) collective-permute-start(f32[34,1,128]{2,1,0:T(1,128)S(1)} %get-tuple-element.13), channel_id=1, source_target_pairs={{0,1},{1,2},{2,3},{3,4},{4,5},{5,6},{6,7},{7,8},{8,9},{9,10},{10,1... | collective-permute-start | bytes 52232 | tf_op jit(solution)/shard_map/ppermute | solution.py:17
  189.3 7.5 %collective-permute-start.15 = (f32[34,1,128]{2,1,0:T(1,128)S(1)}, f32[34,1,128]{2,1,0:T(1,128)S(1)}, u32[]{:S(2)}, u32[]{:S(2)}) collective-permute-start(f32[34,1,128]{2,1,0:T(1,128)S(1)} %get-tuple-element.14), channel_id=1, source_target_pairs={{1,0},{2,1},{3,2},{4,3},{5,4},{6,5},{7,6},{8,7},{9,8},{10,9},{11,1... | collective-permute-start | bytes 52232 | tf_op jit(solution)/shard_map/ppermute | solution.py:18
  236.2 112.8 %collective-permute-start.22 = (bf16[32,8]{0,1:T(8,128)(2,1)S(1)}, bf16[32,8]{0,1:T(8,128)(2,1)S(1)}, u32[]{:S(2)}, u32[]{:S(2)}) collective-permute-start(bf16[32,8]{0,1:T(8,128)(2,1)S(1)} %bitcast.260), channel_id=1, source_target_pairs={{32,0},{64,32},{96,64},{128,96},{160,128},{192,160},{224,192},{256... | collective-permute-start | bytes 1544 | tf_op jit(solution)/shard_map/ppermute | solution.py:26
  246.6 92.4 %collective-permute-start.23 = (bf16[32,8]{0,1:T(8,128)(2,1)S(1)}, bf16[32,8]{0,1:T(8,128)(2,1)S(1)}, u32[]{:S(2)}, u32[]{:S(2)}) collective-permute-start(bf16[32,8]{0,1:T(8,128)(2,1)S(1)} %bitcast.261), channel_id=1, source_target_pairs={{64,0},{96,32},{128,64},{160,96},{192,128},{224,160},{256,192},{28... | collective-permute-start | bytes 1544 | tf_op jit(solution)/shard_map/ppermute | solution.py:26
  247.9 90.6 %collective-permute-start.21 = (bf16[32,8]{0,1:T(8,128)(2,1)S(1)}, bf16[32,8]{0,1:T(8,128)(2,1)S(1)}, u32[]{:S(2)}, u32[]{:S(2)}) collective-permute-start(bf16[32,8]{0,1:T(8,128)(2,1)S(1)} %bitcast.262), channel_id=1, source_target_pairs={{0,32},{32,64},{64,96},{96,128},{128,160},{160,192},{192,224},{224... | collective-permute-start | bytes 1544 | tf_op jit(solution)/shard_map/ppermute | solution.py:26
  251.6 87.2 %collective-permute-start.20 = (bf16[32,8]{0,1:T(8,128)(2,1)S(1)}, bf16[32,8]{0,1:T(8,128)(2,1)S(1)}, u32[]{:S(2)}, u32[]{:S(2)}) collective-permute-start(bf16[32,8]{0,1:T(8,128)(2,1)S(1)} %bitcast.263), channel_id=1, source_target_pairs={{0,64},{32,96},{64,128},{96,160},{128,192},{160,224},{192,256},{22... | collective-permute-start | bytes 1544 | tf_op jit(solution)/shard_map/ppermute | solution.py:26
  290.5 16.2 %collective-permute-start.17 = (bf16[32,8,128]{2,0,1:T(8,128)(2,1)S(1)}, bf16[32,8,128]{2,0,1:T(8,128)(2,1)S(1)}, u32[]{:S(2)}, u32[]{:S(2)}) collective-permute-start(bf16[32,8,128]{2,0,1:T(8,128)(2,1)S(1)} %copy.47), channel_id=1, source_target_pairs={{0,32},{32,64},{64,96},{96,128},{128,160},{160,192},{192,224},{224... | collective-permute-start | bytes 196616 | tf_op jit(solution)/shard_map/ppermute | solution.py:26
  306.6 2.9 collective-permute-start.16
  309.6 5.3 %collective-permute-start.19 = (bf16[32,8,128]{2,0,1:T(8,128)(2,1)S(1)}, bf16[32,8,128]{2,0,1:T(8,128)(2,1)S(1)}, u32[]{:S(2)}, u32[]{:S(2)}) collective-permute-start(bf16[32,8,128]{2,0,1:T(8,128)(2,1)S(1)} %copy.47), channel_id=1, source_target_pairs={{64,0},{96,32},{128,64},{160,96},{192,128},{224,160},{256,192},{28... | collective-permute-start | bytes 196616 | tf_op jit(solution)/shard_map/ppermute | solution.py:26
  314.9 10.2 %collective-permute-start.18 = (bf16[32,8,128]{2,0,1:T(8,128)(2,1)S(1)}, bf16[32,8,128]{2,0,1:T(8,128)(2,1)S(1)}, u32[]{:S(2)}, u32[]{:S(2)}) collective-permute-start(bf16[32,8,128]{2,0,1:T(8,128)(2,1)S(1)} %copy.47), channel_id=1, source_target_pairs={{32,0},{64,32},{96,64},{128,96},{160,128},{192,160},{224,192},{256... | collective-permute-start | bytes 196616 | tf_op jit(solution)/shard_map/ppermute | solution.py:26
  (3 other events, 13.7 us)
where the time goes:
time: 354 us; the launch traced here: 353 us
  blocking collectives  125 us (35%)
  starting transfers between devices  119 us (34%)
  other arithmetic  61.2 us (17%)
  waiting for transfers between devices  23.8 us (7%)
  matrix products  13.2 us (4%)
  local copies, waits for them, and re-layouts  10 us (3%)
    ppermute x16, starting transfers between devices, shifted(): return lax.ppermute(block, axis, route)  90.4 us
    all_gather x2, blocking collectives, local(): lax.all_gather(scaled[None], 'lon', axis=0, tiled=True)  70.6 us
    all_gather x2, blocking collectives, local(): lax.all_gather(innov[None], 'lon', axis=0, tiled=True)  54.2 us
    another operation x6, other arithmetic, square_root(): factor = jnp.linalg.cholesky(system)  24.8 us
    ppermute x4, starting transfers between devices, with_halo(): after = lax.ppermute(first, axis, down)  23.9 us
    another operation x4, other arithmetic, square_root(): inverse = jax.scipy.linalg.solve_triangular(factor, eye, lower=True)  21 us
    ppermute x16, waiting for transfers between devices, shifted(): return lax.ppermute(block, axis, route)  18.5 us
    select_n x2, other arithmetic, local(): padded = jnp.where(cut_top | cut_bottom, 0.0, padded)  8.69 us
  transfers between devices with their start and end apart: 24, of which 13 were waited for; matrix products, arithmetic and copies ran while one was open for 16% of the time, Pallas kernels for 0%

commit v1 on v0

v1 whole, which is shorter than its diff:
```python
import functools
import math
import jax
import jax.numpy as jnp
from jax import lax
from jax.experimental import pallas as pl
from jax.experimental.pallas import tpu as pltpu
from jax.sharding import PartitionSpec as P

MESH = pl.DeviceIdType.MESH
F32 = jnp.float32
BF16 = jnp.bfloat16
ROWS, COLS, N = 32, 128, 128
SLOTS = 8
LATS, LONS = 24, 32
YS, XS = 8, 4
TOP, BOTTOM, LEFT, RIGHT, BLANK = 0, COLS + 2, 2 * (COLS + 2), 2 * (COLS + 2) + ROWS, 2 * (COLS + 2) + 2 * ROWS
RIM = BLANK + 1
NB = N // 8
NEAR = (-2, -1, 1, 2)
VMEM_BYTES = 48 * 2**20


def split3(x):
    high = x.astype(BF16).astype(F32)
    rest = x - high
    mid = rest.astype(BF16).astype(F32)
    return high, mid, rest - mid


def outer8(r, g):
    rh, rm, rl = split3(r)
    gh, gm, gl = split3(g)
    lhs = jnp.concatenate([rh, rh, rm, rh, rl, rm], axis=0).astype(BF16)
    rhs = jnp.concatenate([gh, gm, gh, gl, gh, gm], axis=0).astype(BF16)
    return lax.dot_general(lhs, rhs, (((0,), (0,)), ((), ())), preferred_element_type=F32)


def spread_row(x, k):
    return jnp.broadcast_to(x[k : k + 1, :], (8, N))


def spread_col(x, c):
    return jnp.broadcast_to(x[:, c : c + 1], (8, N))


def transform_t(gram, proj):
    lane = lax.broadcasted_iota(jnp.int32, (8, N), 1)
    sub = lax.broadcasted_iota(jnp.int32, (8, N), 0)
    prow = jnp.broadcast_to(proj, (8, N))
    w = [gram[8 * i : 8 * i + 8, :] + jnp.where(lane == sub + 8 * i, N - 1.0, 0.0) for i in range(NB)]
    inverse, sums = [], []
    acc = jnp.zeros((8, N), F32)
    for j in range(NB):
        c0 = 8 * j
        wj = w[j]
        cols = [spread_col(wj, c0 + k) for k in range(8)]
        here = (lane >= c0) & (lane < c0 + 8)
        f = jnp.where(here, jnp.where(lane == sub + c0, 1.0, 0.0), wj)
        lower, diag = f, cols[0]
        for k in range(8):
            inv = 1.0 / spread_row(cols[k], k)
            if k:
                lower = jnp.where(sub == k, f, lower)
                diag = jnp.where(sub == k, cols[k], diag)
            m = jnp.where(sub == k, 0.0, cols[k] * inv)
            for t in range(k + 1, 8):
                cols[t] = cols[t] - m * spread_row(cols[t], k)
            f = f - m * spread_row(f, k)
        g = f * (1.0 / diag)
        lj = jnp.where(lane <= c0 + 7, lower * lax.rsqrt(diag), 0.0)
        inverse.append(lj)
        sums.append(jnp.sum(lj, axis=1, keepdims=True))
        acc = acc + lj * jnp.sum(lj * prow, axis=1, keepdims=True)
        if j < NB - 1:
            nxt = w[j + 1]
            upd = jnp.where(here, 0.0, nxt)
            for k in range(8):
                upd = upd - spread_col(nxt, c0 + k) * spread_row(g, k)
            if j < NB - 2:
                p = outer8(wj, g)
                for i in range(j + 2, NB):
                    w[i] = jnp.where(here, 0.0, w[i]) - p[8 * i : 8 * i + 8, :]
            w[j + 1] = upd
    weights = jnp.sum(acc, axis=0, keepdims=True)
    total = jnp.sum(weights, axis=1, keepdims=True)
    root = math.sqrt(N - 1.0)
    out = []
    for i in range(NB):
        fix = (1.0 - (root * sums[i] + total)) * (1.0 / N)
        out.append(root * inverse[i] + weights + fix)
    return jnp.concatenate(out, axis=0)


def times(x, tt):
    return lax.dot_general(
        x, tt, (((1,), (1,)), ((), ())), precision=lax.Precision.HIGHEST, preferred_element_type=F32
    )


def position():
    lat, lon = lax.axis_index("lat"), lax.axis_index("lon")
    return lat, lon, lon // YS, lax.rem(lon, YS)


def inside(lat, step):
    return (lat + step >= 0) & (lat + step < LATS)


def enter(lat, lon, x, y):
    barrier = pltpu.get_barrier_semaphore()

    def greet(a, c):
        pl.semaphore_signal(barrier, inc=1, device_id=(a, c), device_id_type=MESH)

    east, west = lax.rem(lon + 1, LONS), lax.rem(lon + LONS - 1, LONS)
    greet(lat, east)
    greet(lat, west)
    for t in range(1, YS):
        greet(lat, x * YS + lax.rem(y + t, YS))
    for t in range(1, XS):
        greet(lat, lax.rem(x + t, XS) * YS + y)
    for step in NEAR:

        @pl.when(inside(lat, step))
        def _():
            greet(lat + step, lon)
            if abs(step) == 1:
                greet(lat + step, east)
                greet(lat + step, west)

    count = YS - 1 + XS - 1 + 2
    for step in NEAR:
        count = count + jnp.where(inside(lat, step), 3 if abs(step) == 1 else 1, 0)
    pl.semaphore_wait(barrier, count)


def masks(batch, pattern_ref, mark, markv):
    @pl.loop(0, 5 * LONS)
    def _(i):
        value = pattern_ref[batch, i // LONS, lax.rem(i, LONS)].astype(F32)
        mark[i] = jnp.full((SLOTS, N), value, F32).astype(BF16)
        markv[i] = jnp.full((1, N), value, F32)


def blank_rows(lat, seen, seenv):
    for step in NEAR:

        @pl.when(jnp.logical_not(inside(lat, step)))
        def _():
            d = step + 2
            seen[pl.ds(d * LONS, LONS)] = jnp.zeros((LONS, SLOTS, N), BF16)
            seenv[pl.ds(d * LONS, LONS)] = jnp.zeros((LONS, 1, N), F32)


def observe(batch, prior, observed_ref, precision_ref, owned_ref):
    sub = lax.broadcasted_iota(jnp.int32, (SLOTS, N), 0)
    obs = jnp.zeros((SLOTS, N), F32)
    prec = jnp.zeros((SLOTS, N), F32)
    own = jnp.zeros((SLOTS, N), F32)
    for o in range(SLOTS):
        obs = jnp.where(sub == o, observed_ref[batch, o], obs)
        prec = jnp.where(sub == o, precision_ref[batch, o], prec)
        own = jnp.where(sub == o, owned_ref[batch, o].astype(F32), own)
    root = jnp.sqrt(prec) * own
    mean = jnp.sum(prior, axis=1, keepdims=True) * (1.0 / N)
    scaled = (root * (prior - mean)).astype(BF16)
    innov = (root * (obs - mean)).astype(BF16)
    vector = jnp.sum(scaled.astype(F32) * innov.astype(F32), axis=0, keepdims=True)
    return scaled, vector


def spread_out(pos, seen, seenv, sems, mark, markv):
    lat, lon, x, y = pos
    mine = 2 * LONS

    def copy(ref, start, size, to, device, sem, slot):
        return pltpu.make_async_remote_copy(
            src_ref=ref.at[pl.ds(start, size)],
            dst_ref=ref.at[pl.ds(to, size)],
            send_sem=sem.at[0, slot],
            recv_sem=sem.at[1, slot],
            device_id=device,
            device_id_type=MESH,
        )

    def both(start, size, to, device, slot):
        return (
            copy(seen, start, size, to, device, sems[0], slot),
            copy(seenv, start, size, to, device, sems[1], slot),
        )

    stage_y = []
    for t in range(1, YS):
        device = (lat, x * YS + lax.rem(y + t, YS))
        stage_y += both(mine + lon, 1, mine + lon, device, t - 1)
    for c in stage_y:
        c.start()
    for c in stage_y:
        c.wait()
    stage_x = []
    for t in range(1, XS):
        device = (lat, lax.rem(x + t, XS) * YS + y)
        stage_x += both(mine + x * YS, YS, mine + x * YS, device, YS - 1 + t - 1)
    for c in stage_x:
        c.start()
    for c in stage_x:
        c.wait()

    def lat_copies(i, step):
        return both(mine, LONS, (2 - step) * LONS, (lat + step, lon), YS + XS - 2 + i)

    for i, step in enumerate(NEAR):

        @pl.when(inside(lat, step))
        def _():
            for c in lat_copies(i, step):
                c.start()

    def term(d):
        rows = seen[pl.ds(d * LONS, LONS)]
        marked = rows * mark[pl.ds(d * LONS, LONS)]
        gram = lax.dot_general(
            marked.reshape(LONS * SLOTS, N),
            rows.reshape(LONS * SLOTS, N),
            (((0,), (0,)), ((), ())),
            preferred_element_type=F32,
        )
        return gram, jnp.sum(seenv[pl.ds(d * LONS, LONS)] * markv[pl.ds(d * LONS, LONS)], axis=0)

    gram, proj = term(2)
    for i, step in enumerate(NEAR):

        @pl.when(inside(lat, step))
        def _():
            for c in lat_copies(i, step):
                c.wait_send()

        @pl.when(inside(lat, -step))
        def _():
            for c in lat_copies(i, step):
                c.wait_recv()

        g, v = term(2 - step)
        gram, proj = gram + g, proj + v
    return gram, proj


def corner(stencil_ref, batch, o):
    s = stencil_ref[batch, 0, o]
    r = s // (COLS + 2)
    return r, s - r * (COLS + 2)


def first_kernel(
    ens, observed, precision, weight, stencil, owned, pattern,
    gram_ref, proj_ref, raw_ref,
    tile, prior, seen, seenv, mark, markv, local_sem, halo_sem, sem_s, sem_v,
):
    pos = position()
    lat, lon, x, y = pos
    east, west = lax.rem(lon + 1, LONS), lax.rem(lon + LONS - 1, LONS)
    inner = pltpu.make_async_copy(ens, tile.at[pl.ds(1, ROWS), pl.ds(1, COLS)], local_sem)
    inner.start()
    for step, r in ((-1, 0), (1, ROWS + 1)):

        @pl.when(jnp.logical_not(inside(lat, step)))
        def _():
            tile[r] = jnp.zeros((COLS + 2, 1, N), F32)

    blank_rows(lat, seen, seenv)
    enter(lat, lon, x, y)

    def halo(src, dst, device, slot):
        return pltpu.make_async_remote_copy(
            src_ref=src, dst_ref=dst, send_sem=halo_sem.at[0, slot], recv_sem=halo_sem.at[1, slot],
            device_id=device, device_id_type=MESH,
        )

    sides = [
        halo(ens.at[:, COLS - 1], tile.at[pl.ds(1, ROWS), 0], (lat, east), 0),
        halo(ens.at[:, 0], tile.at[pl.ds(1, ROWS), COLS + 1], (lat, west), 1),
    ]

    def ends(step):
        r, to, slot = (ROWS - 1, 0, 2) if step == 1 else (0, ROWS + 1, 5)
        return [
            halo(ens.at[r], tile.at[to, pl.ds(1, COLS)], (lat + step, lon), slot),
            halo(ens.at[r, COLS - 1], tile.at[to, 0], (lat + step, east), slot + 1),
            halo(ens.at[r, 0], tile.at[to, COLS + 1], (lat + step, west), slot + 2),
        ]

    for step in (1, -1):

        @pl.when(inside(lat, step))
        def _():
            for c in ends(step):
                c.start()

    for c in sides:
        c.start()
    masks(0, pattern, mark, markv)
    inner.wait()
    for c in sides:
        c.wait()
    for step in (1, -1):

        @pl.when(inside(lat, step))
        def _():
            for c in ends(step):
                c.wait_send()

        @pl.when(inside(lat, -step))
        def _():
            for c in ends(step):
                c.wait_recv()

    for o in range(SLOTS):
        r, c = corner(stencil, 0, o)
        total = jnp.zeros((1, N), F32)
        for k in range(4):
            total = total + weight[0, k, o] * tile[r + k // 2, c + k % 2]
        prior[pl.ds(o, 1), :] = total
    for o in range(SLOTS):
        r, c = corner(stencil, 1, o)
        total = jnp.zeros((1, N), F32)
        for k in range(4):
            rk, ck = r + k // 2, c + k % 2
            own = (rk >= 1) & (rk <= ROWS) & (ck >= 1) & (ck <= COLS)
            total = total + jnp.where(own, weight[1, k, o], 0.0) * tile[rk, ck]
        raw_ref[pl.ds(o, 1), :] = total
    scaled, vector = observe(0, prior[...], observed, precision, owned)
    seen[2 * LONS + lon] = scaled
    seenv[2 * LONS + lon] = vector
    gram_ref[...], proj_ref[...] = spread_out(pos, seen, seenv, (sem_s, sem_v), mark, markv)


def second_kernel(
    rows_ref, sides_ref, held, observed, precision, weight, stencil, owned, pattern,
    gram_ref, proj_ref,
    rim, prior, seen, seenv, mark, markv, halo_sem, sem_s, sem_v,
):
    pos = position()
    lat, lon, x, y = pos
    east, west = lax.rem(lon + 1, LONS), lax.rem(lon + LONS - 1, LONS)
    rim[BLANK] = jnp.zeros((1, N), F32)
    for step, r in ((-1, TOP), (1, BOTTOM)):

        @pl.when(jnp.logical_not(inside(lat, step)))
        def _():
            rim[pl.ds(r, COLS + 2)] = jnp.zeros((COLS + 2, 1, N), F32)

    blank_rows(lat, seen, seenv)
    enter(lat, lon, x, y)

    def halo(src, dst, device, slot):
        return pltpu.make_async_remote_copy(
            src_ref=src, dst_ref=dst, send_sem=halo_sem.at[0, slot], recv_sem=halo_sem.at[1, slot],
            device_id=device, device_id_type=MESH,
        )

    sides = [
        halo(sides_ref.at[1], rim.at[pl.ds(LEFT, ROWS)], (lat, east), 0),
        halo(sides_ref.at[0], rim.at[pl.ds(RIGHT, ROWS)], (lat, west), 1),
    ]

    def ends(step):
        r, to, slot = (1, TOP, 2) if step == 1 else (0, BOTTOM, 5)
        return [
            halo(rows_ref.at[r], rim.at[pl.ds(to + 1, COLS)], (lat + step, lon), slot),
            halo(rows_ref.at[r, pl.ds(COLS - 1, 1)], rim.at[pl.ds(to, 1)], (lat + step, east), slot + 1),
            halo(rows_ref.at[r, pl.ds(0, 1)], rim.at[pl.ds(to + COLS + 1, 1)], (lat + step, west), slot + 2),
        ]

    for step in (1, -1):

        @pl.when(inside(lat, step))
        def _():
            for c in ends(step):
                c.start()

    for c in sides:
        c.start()
    masks(1, pattern, mark, markv)
    for c in sides:
        c.wait()
    for step in (1, -1):

        @pl.when(inside(lat, step))
        def _():
            for c in ends(step):
                c.wait_send()

        @pl.when(inside(lat, -step))
        def _():
            for c in ends(step):
                c.wait_recv()

    for o in range(SLOTS):
        r, c = corner(stencil, 1, o)
        total = held[pl.ds(o, 1), :]
        for k in range(4):
            rk, ck = r + k // 2, c + k % 2
            where = jnp.where(ck == 0, LEFT - 1 + rk, jnp.where(ck == COLS + 1, RIGHT - 1 + rk, BLANK))
            where = jnp.where(rk == 0, TOP + ck, jnp.where(rk == ROWS + 1, BOTTOM + ck, where))
            total = total + weight[1, k, o] * rim[where]
        prior[pl.ds(o, 1), :] = total
    scaled, vector = observe(1, prior[...], observed, precision, owned)
    seen[2 * LONS + lon] = scaled
    seenv[2 * LONS + lon] = vector
    gram_ref[...], proj_ref[...] = spread_out(pos, seen, seenv, (sem_s, sem_v), mark, markv)


def between_kernel(gram, proj, raw, ens, ens_cells, tt_ref, held_ref, rows_ref, sides_ref, edge, strip, sems):
    copies = [
        pltpu.make_async_copy(ens.at[0], edge.at[0], sems.at[0]),
        pltpu.make_async_copy(ens.at[ROWS - 1], edge.at[1], sems.at[1]),
        pltpu.make_async_copy(ens_cells.at[:, 0], strip.at[0], sems.at[2]),
        pltpu.make_async_copy(ens_cells.at[:, COLS - 1], strip.at[1], sems.at[3]),
    ]
    for c in copies:
        c.start()
    tt = transform_t(gram[...], proj[...])
    tt_ref[...] = tt
    for c in copies:
        c.wait()
    held_ref[...] = times(raw[...], tt)
    for i in range(2):
        rows_ref[i] = times(edge[i], tt).reshape(COLS, 1, N)
        sides_ref[i] = times(strip[i].reshape(ROWS, N), tt).reshape(ROWS, 1, N)


CHUNK = 512


def last_kernel(gram, proj, tt_ref, ens, out, cells, moved, in_sem, out_sem):
    chunks = ROWS * COLS // CHUNK
    loads = [
        pltpu.make_async_copy(ens.at[pl.ds(i * CHUNK, CHUNK)], cells.at[pl.ds(i * CHUNK, CHUNK)], in_sem.at[i])
        for i in range(chunks)
    ]
    for c in loads:
        c.start()
    tt = transform_t(gram[...], proj[...])
    both = jnp.dot(tt, tt_ref[...], precision=lax.Precision.HIGHEST, preferred_element_type=F32)
    high = both.astype(BF16)
    low = (both - high.astype(F32)).astype(BF16)
    right = jnp.concatenate(
        [jnp.concatenate([high, high], axis=1), jnp.concatenate([low, jnp.zeros_like(low)], axis=1)], axis=0
    )
    stores = []
    for i in range(chunks):
        rows = pl.ds(i * CHUNK, CHUNK)
        loads[i].wait()
        xs = cells[rows, :]
        xh = xs.astype(BF16)
        xl = (xs - xh.astype(F32)).astype(BF16)
        res = lax.dot_general(
            jnp.concatenate([xh, xl], axis=1), right, (((1,), (1,)), ((), ())), preferred_element_type=F32
        )
        moved[rows, :] = res[:, :N] + res[:, N:]
        c = pltpu.make_async_copy(moved.at[rows], out.at[rows], out_sem.at[i])
        c.start()
        stores.append(c)
    for c in stores:
        c.wait()


def shape(*dims):
    return jax.ShapeDtypeStruct(dims, F32)


VM = pl.BlockSpec(memory_space=pltpu.VMEM)
SM = pl.BlockSpec(memory_space=pltpu.SMEM)
ANY = pl.BlockSpec(memory_space=pl.ANY)


def exchange_scratch():
    return [
        pltpu.VMEM((SLOTS, N), F32),
        pltpu.VMEM((5 * LONS, SLOTS, N), BF16),
        pltpu.VMEM((5 * LONS, 1, N), F32),
        pltpu.VMEM((5 * LONS, SLOTS, N), BF16),
        pltpu.VMEM((5 * LONS, 1, N), F32),
    ]


def exchange_sems():
    count = YS - 1 + XS - 1 + len(NEAR)
    return [
        pltpu.SemaphoreType.DMA((2, 8)),
        pltpu.SemaphoreType.DMA((2, count)),
        pltpu.SemaphoreType.DMA((2, count)),
    ]


def local(ensemble, observed, precision, interp_weight, stencil, owned, pattern):
    cells = ensemble.reshape(ROWS, COLS, 1, N)
    small = (
        observed.reshape(2, SLOTS),
        precision.reshape(2, SLOTS),
        interp_weight.reshape(2, 4, SLOTS),
        stencil.reshape(2, 4, SLOTS),
        owned.reshape(2, SLOTS),
        pattern.reshape(2, 5, LONS),
    )
    gram, proj, raw = pl.pallas_call(
        first_kernel,
        out_shape=(shape(N, N), shape(1, N), shape(SLOTS, N)),
        in_specs=[ANY] + [SM] * 6,
        out_specs=(VM, VM, VM),
        scratch_shapes=[pltpu.VMEM((ROWS + 2, COLS + 2, 1, N), F32)]
        + exchange_scratch()
        + [pltpu.SemaphoreType.DMA]
        + exchange_sems(),
        compiler_params=pltpu.CompilerParams(collective_id=0, has_side_effects=True, vmem_limit_bytes=VMEM_BYTES),
        name="first",
    )(cells, *small)
    tt, held, rows, sides = pl.pallas_call(
        between_kernel,
        out_shape=(shape(N, N), shape(SLOTS, N), shape(2, COLS, 1, N), shape(2, ROWS, 1, N)),
        in_specs=[VM, VM, VM, ANY, ANY],
        out_specs=(VM, VM, VM, VM),
        scratch_shapes=[
            pltpu.VMEM((2, COLS, N), F32),
            pltpu.VMEM((2, ROWS, 1, N), F32),
            pltpu.SemaphoreType.DMA((4,)),
        ],
        compiler_params=pltpu.CompilerParams(vmem_limit_bytes=VMEM_BYTES),
        name="between",
    )(gram, proj, raw, ensemble, cells)
    gram, proj = pl.pallas_call(
        second_kernel,
        out_shape=(shape(N, N), shape(1, N)),
        in_specs=[VM, VM, VM] + [SM] * 6,
        out_specs=(VM, VM),
        scratch_shapes=[pltpu.VMEM((RIM, 1, N), F32)] + exchange_scratch() + exchange_sems(),
        compiler_params=pltpu.CompilerParams(collective_id=1, has_side_effects=True, vmem_limit_bytes=VMEM_BYTES),
        name="second",
    )(rows, sides, held, *small)
    chunks = ROWS * COLS // CHUNK
    out = pl.pallas_call(
        last_kernel,
        out_shape=shape(ROWS * COLS, N),
        in_specs=[VM, VM, VM, ANY],
        out_specs=ANY,
        scratch_shapes=[
            pltpu.VMEM((ROWS * COLS, N), F32),
            pltpu.VMEM((ROWS * COLS, N), F32),
            pltpu.SemaphoreType.DMA((chunks,)),
            pltpu.SemaphoreType.DMA((chunks,)),
        ],
        compiler_params=pltpu.CompilerParams(vmem_limit_bytes=VMEM_BYTES),
        name="last",
    )(gram, proj, tt, ensemble.reshape(ROWS * COLS, N))
    return out.reshape(ROWS, COLS, N)


def solution(mesh):
    placed = (
        P("lat", "lon", None),
        P(None, "lat", "lon", None),
        P(None, "lat", "lon", None),
        P(None, "lat", "lon", None, None),
        P(None, "lat", "lon", None, None),
        P(None, "lat", "lon", None),
        P(None, "lat", "lon", None, None),
    )
    return jax.shard_map(
        local, mesh=mesh, in_specs=placed, out_specs=P("lat", "lon", None), check_vma=False
    )
```

time: 354 us -> 72.6 us (0.21)
  blocking collectives: 125 us -> 0 us
  starting transfers between devices: 119 us -> 0 us
  Pallas kernels: 0 us -> 66.5 us
  other arithmetic: 61.2 us -> 0 us
  waiting for transfers between devices: 23.8 us -> 0 us
  matrix products: 13.2 us -> 0 us
  local copies, waits for them, and re-layouts: 10 us -> 5.71 us
    all_gather x4 -> x0, blocking collectives: 125 us -> none  [the longest x2 70.6 us: local(): lax.all_gather(scaled[None], 'lon', axis=0, tiled=True)]
    ppermute x24 -> x0, starting transfers between devices: 119 us -> none  [the longest x16 90.4 us: shifted(): return lax.ppermute(block, axis, route)]
    pallas_call x0 -> x4, Pallas kernels: none -> 66.5 us  [the longest x1 30.5 us: local(): pl.pallas_call(first_kernel, out_shape=(shape(N, N), shape(1, N), shape(S...]
    another operation x11 -> x0, other arithmetic: 46.4 us -> none  [the longest x6 24.8 us: square_root(): factor = jnp.linalg.cholesky(system)]
    ppermute x24 -> x0, waiting for transfers between devices: 23.8 us -> none  [the longest x16 18.5 us: shifted(): return lax.ppermute(block, axis, route)]
    dot_general x22 -> x0, matrix products: 11.8 us -> none  [the longest x2 7.33 us: local(): jnp.dot(spread, transform, precision=lax.Precision.HIGHEST, preferred_ele...]
    select_n x3 -> x0, other arithmetic: 9.39 us -> none  [the longest x2 8.69 us: local(): padded = jnp.where(cut_top | cut_bottom, 0.0, padded)]
    unnamed x9 -> x17, local copies, waits for them, and re-layouts: 0.2 us -> 5.7 us
  transfers between devices with their start and end apart: 24 -> 0, of which waited for: 13 -> 0; matrix products, arithmetic and copies ran while one was open for 16% -> 0% of each run, Pallas kernels for 0% -> 0%
where the time goes in v1:
time: 72.6 us; the launch traced here: 72.3 us
  Pallas kernels  66.5 us (92%)
  local copies, waits for them, and re-layouts  5.71 us (8%)
    pallas_call x1, Pallas kernels, local(): pl.pallas_call(first_kernel, out_shape=(shape(N, N), shape(1, N), shape(S...  30.5 us
    pallas_call x1, Pallas kernels, local(): pl.pallas_call(second_kernel, out_shape=(shape(N, N), shape(1, N)), in_sp...  24.1 us
    pallas_call x1, Pallas kernels, local(): pl.pallas_call(last_kernel, out_shape=shape(ROWS * COLS, N), in_specs=[VM...  7.33 us
    unnamed x17, local copies, waits for them, and re-layouts  5.7 us
    pallas_call x1, Pallas kernels, local(): pl.pallas_call(between_kernel, out_shape=(shape(N, N), shape(SLOTS, N), s...  4.58 us

profile of v1, /device:TPU:1, one launch (start us, length us, event | category | flops | bytes accessed | tf_op | source)
XLA Modules:
  0.0 72.3 jit_solution(2723565749287500616)
XLA Ops:
  0.0 0.7 copy.12
  0.7 0.0 copy-start
  0.7 1.6 %copy-done = f32[32,128,128]{2,1,0:T(8,128)S(1)} copy-done((f32[32,128,128]{2,1,0:T(8,128)S(1)}, f32[32,128,128]{2,1,0:T(8,128)}, u32[]{:S(2)}) %copy-start) | copy-done | bytes 2097176
  2.3 0.0 copy-start.2
  2.3 0.7 copy-done.2
  3.0 0.0 copy-start.3
  3.0 0.7 copy-done.3
  3.7 0.0 copy-start.4
  3.7 0.7 copy-done.4
  4.3 0.0 copy-start.5
  4.3 0.7 copy-done.5
  5.0 0.0 copy-start.6
  5.0 0.7 copy-done.6
  5.7 30.5 %first.1 = (f32[128,128]{1,0:T(8,128)S(1)}, f32[1,128]{1,0:T(1,128)S(1)}, f32[8,128]{1,0:T(8,128)S(1)}) custom-call(f32[32,128,1,128]{3,2,1,0:T(1,128)S(1)} %bitcast.11, f32[2,8]{1,0:T(2,128)S(1)} %bitcast.18, f32[2,8]{1,0:T(2,128)S(1)} %bitcast.20, f32[2,4,8]{2,1,0:T(4,128)S(1)} %bitcast.14, s32[2,4,8]{2,1,0:T(4,128)S(1)} %bitcast.16, s32[2,8]{1,0:T(2,128)S(1)} %bitcast.22, ...), custom_call_target="tpu_custom_call" | custom-call | tf_op jit(solution)/shard_map/first/pallas_call | solution.py:507
  36.2 0.0 copy-start.7
  36.3 0.0 copy-start.1
  36.3 4.6 %between.1 = (f32[128,128]{1,0:T(8,128)S(1)}, f32[8,128]{1,0:T(8,128)S(1)}, f32[2,128,1,128]{3,2,1,0:T(1,128)S(1)}, f32[2,32,1,128]{3,2,1,0:T(1,128)S(1)}) custom-call(f32[128,128]{1,0:T(8,128)S(1)} %get-tuple-element.14.gram, f32[1,128]{1,0:T(1,128)S(1)} %get-tuple-element.15.proj, f32[8,128]{1,0:T(8,128)S(1)} %get-tuple-element.16.raw, ...), custom_call_target="tpu_custom_call" | custom-call | tf_op jit(solution)/shard_map/between/pallas_call | solution.py:519
  40.8 0.0 copy-done.7
  40.9 24.1 %second.1 = (f32[128,128]{1,0:T(8,128)S(1)}, f32[1,128]{1,0:T(1,128)S(1)}) custom-call(f32[2,128,1,128]{3,2,1,0:T(1,128)S(1)} %get-tuple-element.17.rows_ref, f32[2,32,1,128]{3,2,1,0:T(1,128)S(1)} %get-tuple-element.18.sides_ref, f32[8,128]{1,0:T(8,128)S(1)} %get-tuple-element.19.held, f32[2,8]{1,0:T(2,128)S(1)} %bitcast.19, f32[2,8]{1,0:T(2,128)S(1)} %bitcast.21, ...), custom_call_target="tpu_custom_call" | custom-call | tf_op jit(solution)/shard_map/second/pallas_call | solution.py:532
  64.9 0.0 copy-done.1
  64.9 7.3 %last.1 = f32[4096,128]{1,0:T(8,128)} custom-call(f32[128,128]{1,0:T(8,128)S(1)} %get-tuple-element.20.gram, f32[1,128]{1,0:T(1,128)S(1)} %get-tuple-element.21.proj, f32[128,128]{1,0:T(8,128)S(1)} %get-tuple-element.22.tt_ref, f32[4096,128]{1,0:T(8,128)S(1)} %bitcast.13), custom_call_target="tpu_custom_call" | custom-call | tf_op jit(solution)/shard_map/last/pallas_call | solution.py:542
  (1 shorter events, 0.0 us)
Async XLA Ops:
  0.7 1.6 %copy-start = (f32[32,128,128]{2,1,0:T(8,128)S(1)}, f32[32,128,128]{2,1,0:T(8,128)}, u32[]{:S(2)}) copy-start(f32[32,128,128]{2,1,0:T(8,128)} %ens.1) | copy-start | bytes 6291460
  2.3 0.7 copy-start.2
  3.0 0.7 copy-start.3
  3.7 0.7 copy-start.4
  4.3 0.7 copy-start.5
  5.0 0.7 copy-start.6
  36.2 4.6 %copy-start.7 = (s32[2,1,1,8]{3,2,1,0:T(1,128)S(1)}, s32[2,1,1,8]{3,2,1,0:T(1,128)}, u32[]{:S(2)}) copy-start(s32[2,1,1,8]{3,2,1,0:T(1,128)} %param.12) | copy-start | bytes 196
  36.3 28.7 %copy-start.1 = (f32[32,128,128]{2,1,0:T(8,128)S(1)}, f32[32,128,128]{2,1,0:T(8,128)}, u32[]{:S(2)}) copy-start(f32[32,128,128]{2,1,0:T(8,128)} %ens.1) | copy-start | bytes 6291460

commit v2 on v1

v2 whole, which is shorter than its diff:
```python
import functools
import math
import jax
import jax.numpy as jnp
from jax import lax
from jax.experimental import pallas as pl
from jax.experimental.pallas import tpu as pltpu
from jax.sharding import PartitionSpec as P

MESH = pl.DeviceIdType.MESH
F32 = jnp.float32
BF16 = jnp.bfloat16
ROWS, COLS, N = 32, 128, 128
SLOTS = 8
LATS, LONS = 24, 32
YS, XS = 8, 4
TOP, BOTTOM, LEFT, RIGHT, BLANK = 0, COLS + 2, 2 * (COLS + 2), 2 * (COLS + 2) + ROWS, 2 * (COLS + 2) + 2 * ROWS
RIM = BLANK + 1
NB = N // 8
NEAR = (-2, -1, 1, 2)
SLOT = sorted(
    ((dx, dy) for dx in (-1, 0, 1, 2) for dy in (-3, -2, -1, 0, 1, 2, 3, 4)), key=lambda p: (abs(p[0]) + abs(p[1]), p)
)
HOPS = [abs(dx) + abs(dy) for dx, dy in SLOT]
CUTS = (0, sum(h <= 2 for h in HOPS), sum(h <= 3 for h in HOPS), sum(h <= 4 for h in HOPS), LONS)
GROUPS = tuple(zip(CUTS[:-1], CUTS[1:]))
VMEM_BYTES = 48 * 2**20


def split3(x):
    high = x.astype(BF16).astype(F32)
    rest = x - high
    mid = rest.astype(BF16).astype(F32)
    return high, mid, rest - mid


def outer8(r, g):
    rh, rm, rl = split3(r)
    gh, gm, gl = split3(g)
    lhs = jnp.concatenate([rh, rh, rm, rh, rl, rm], axis=0).astype(BF16)
    rhs = jnp.concatenate([gh, gm, gh, gl, gh, gm], axis=0).astype(BF16)
    return lax.dot_general(lhs, rhs, (((0,), (0,)), ((), ())), preferred_element_type=F32)


def spread_row(x, k):
    return jnp.broadcast_to(x[k : k + 1, :], (8, N))


def spread_col(x, c):
    return jnp.broadcast_to(x[:, c : c + 1], (8, N))


def transform_t(gram, proj):
    lane = lax.broadcasted_iota(jnp.int32, (8, N), 1)
    sub = lax.broadcasted_iota(jnp.int32, (8, N), 0)
    prow = jnp.broadcast_to(proj, (8, N))
    w = [gram[8 * i : 8 * i + 8, :] + jnp.where(lane == sub + 8 * i, N - 1.0, 0.0) for i in range(NB)]
    inverse, sums = [], []
    acc = jnp.zeros((8, N), F32)
    for j in range(NB):
        c0 = 8 * j
        wj = w[j]
        cols = [spread_col(wj, c0 + k) for k in range(8)]
        here = (lane >= c0) & (lane < c0 + 8)
        f = jnp.where(here, jnp.where(lane == sub + c0, 1.0, 0.0), wj)
        lower, diag = f, cols[0]
        for k in range(8):
            inv = 1.0 / spread_row(cols[k], k)
            if k:
                lower = jnp.where(sub == k, f, lower)
                diag = jnp.where(sub == k, cols[k], diag)
            m = jnp.where(sub == k, 0.0, cols[k] * inv)
            for t in range(k + 1, 8):
                cols[t] = cols[t] - m * spread_row(cols[t], k)
            f = f - m * spread_row(f, k)
        g = f * (1.0 / diag)
        lj = jnp.where(lane <= c0 + 7, lower * lax.rsqrt(diag), 0.0)
        inverse.append(lj)
        sums.append(jnp.sum(lj, axis=1, keepdims=True))
        acc = acc + lj * jnp.sum(lj * prow, axis=1, keepdims=True)
        if j < NB - 1:
            nxt = w[j + 1]
            upd = jnp.where(here, 0.0, nxt)
            for k in range(8):
                upd = upd - spread_col(nxt, c0 + k) * spread_row(g, k)
            if j < NB - 2:
                p = outer8(wj, g)
                for i in range(j + 2, NB):
                    w[i] = jnp.where(here, 0.0, w[i]) - p[8 * i : 8 * i + 8, :]
            w[j + 1] = upd
    weights = jnp.sum(acc, axis=0, keepdims=True)
    total = jnp.sum(weights, axis=1, keepdims=True)
    root = math.sqrt(N - 1.0)
    out = []
    for i in range(NB):
        fix = (1.0 - (root * sums[i] + total)) * (1.0 / N)
        out.append(root * inverse[i] + weights + fix)
    return jnp.concatenate(out, axis=0)


def times(x, tt):
    return lax.dot_general(
        x, tt, (((1,), (1,)), ((), ())), precision=lax.Precision.HIGHEST, preferred_element_type=F32
    )


def position():
    lat, lon = lax.axis_index("lat"), lax.axis_index("lon")
    return lat, lon, lon // YS, lax.rem(lon, YS)


def inside(lat, step):
    return (lat + step >= 0) & (lat + step < LATS)


def east_west(lon):
    return lax.rem(lon + 1, LONS), lax.rem(lon + LONS - 1, LONS)


def lon_at(x, y, dx, dy):
    return lax.rem(x + dx + XS, XS) * YS + lax.rem(y + dy + YS, YS)


def enter(pos):
    lat, lon, x, y = pos
    barrier = pltpu.get_barrier_semaphore()

    def greet(a, c):
        pl.semaphore_signal(barrier, inc=1, device_id=(a, c), device_id_type=MESH)

    east, west = east_west(lon)
    for step in NEAR:

        @pl.when(inside(lat, step))
        def _():
            greet(lat + step, lon)
            if abs(step) == 1:
                greet(lat + step, east)
                greet(lat + step, west)

    greet(lat, east)
    greet(lat, west)
    for dx, dy in SLOT[:0:-1]:
        greet(lat, lon_at(x, y, -dx, -dy))
    count = LONS - 1 + 2
    for step in NEAR:
        count = count + jnp.where(inside(lat, step), 3 if abs(step) == 1 else 1, 0)
    pl.semaphore_wait(barrier, count)


def masks(pos, batch, pattern_ref, mark, markv):
    lat, lon, x, y = pos

    @pl.loop(0, 5)
    def _(d):
        for i, (dx, dy) in enumerate(SLOT):
            value = pattern_ref[batch, d, 0, lon_at(x, y, dx, dy)].astype(F32)
            mark[d, i] = jnp.full((SLOTS, N), value, F32).astype(BF16)
            markv[d, i] = jnp.full((1, N), value, F32)


def observe(batch, prior, observed_ref, precision_ref, owned_ref):
    sub = lax.broadcasted_iota(jnp.int32, (SLOTS, N), 0)
    obs = jnp.zeros((SLOTS, N), F32)
    prec = jnp.zeros((SLOTS, N), F32)
    own = jnp.zeros((SLOTS, N), F32)
    for o in range(SLOTS):
        obs = jnp.where(sub == o, observed_ref[batch, 0, o], obs)
        prec = jnp.where(sub == o, precision_ref[batch, 0, o], prec)
        own = jnp.where(sub == o, owned_ref[batch, 0, o].astype(F32), own)
    root = jnp.sqrt(prec) * own
    mean = jnp.sum(prior, axis=1, keepdims=True) * (1.0 / N)
    scaled = (root * (prior - mean)).astype(BF16)
    innov = (root * (obs - mean)).astype(BF16)
    vector = jnp.sum(scaled.astype(F32) * innov.astype(F32), axis=0, keepdims=True)
    return scaled, vector


class Exchange:
    def __init__(self, pos, seen, seenv, sems):
        self.pos, self.refs, self.sems = pos, (seen, seenv), (sems.at[0], sems.at[1])

    def pair(self, src, size, dst, device, send, recv):
        (sd, si), (dd, di) = src, dst
        return [
            pltpu.make_async_remote_copy(
                src_ref=ref.at[sd, pl.ds(si, size)], dst_ref=ref.at[dd, pl.ds(di, size)],
                send_sem=sem.at[send], recv_sem=sem.at[recv], device_id=device, device_id_type=MESH,
            )
            for ref, sem in zip(self.refs, self.sems)
        ]

    def blank(self):
        lat = self.pos[0]
        for step in NEAR:

            @pl.when(jnp.logical_not(inside(lat, step)))
            def _():
                for ref in self.refs:
                    ref[step + 2] = jnp.zeros(ref.shape[1:], ref.dtype)

    def row(self, i, g):
        lat, _, x, y = self.pos
        dx, dy = SLOT[i]
        return self.pair((2, 0), 1, (2, i), (lat, lon_at(x, y, -dx, -dy)), 0, 1 + g)

    def row_group(self, g):
        start, stop = max(GROUPS[g][0], 1), GROUPS[g][1]
        return self.pair((2, start), stop - start, (2, start), self.pos[:2], 0, 1 + g)

    def relay(self, k, start, stop):
        lat, lon = self.pos[:2]
        send = 1 + len(GROUPS) + k
        return self.pair(
            (2, start), stop - start, (2 - NEAR[k], start), (lat + NEAR[k], lon), send, send + len(NEAR)
        )

    def start(self, scaled, vector):
        self.refs[0][2, 0] = scaled
        self.refs[1][2, 0] = vector
        for g, (start, stop) in reversed(tuple(enumerate(GROUPS))):
            for i in reversed(range(max(start, 1), stop)):
                for c in self.row(i, g):
                    c.start()

    def finish(self, mark, markv):
        lat = self.pos[0]
        seen, seenv = self.refs

        def term(d):
            rows = seen[d]
            marked = rows * mark[d]
            gram = lax.dot_general(
                marked.reshape(LONS * SLOTS, N),
                rows.reshape(LONS * SLOTS, N),
                (((0,), (0,)), ((), ())),
                preferred_element_type=F32,
            )
            return gram, jnp.sum(seenv[d] * markv[d], axis=0)

        for g, (start, stop) in enumerate(GROUPS):
            for c in self.row_group(g):
                c.wait_recv()
            for k, step in enumerate(NEAR):

                @pl.when(inside(lat, step))
                def _():
                    for c in self.relay(k, start, stop):
                        c.start()

        gram, proj = term(2)
        for k, step in enumerate(NEAR):

            @pl.when(inside(lat, -step))
            def _():
                for c in self.relay(k, 0, LONS):
                    c.wait_recv()

            more, morev = term(2 - step)
            gram, proj = gram + more, proj + morev
        return gram, proj

    def drain(self):
        for c in self.pair((2, 1), LONS - 1, (2, 1), self.pos[:2], 0, 1):
            c.wait_send()
        for k, step in enumerate(NEAR):

            @pl.when(inside(self.pos[0], step))
            def _():
                for c in self.relay(k, 0, LONS):
                    c.wait_send()


class Halo:
    def __init__(self, pos, sems, rows, ends, sides, targets):
        self.pos, self.sems, self.rows, self.ends, self.sides, self.targets = pos, sems, rows, ends, sides, targets

    def copy(self, src, dst, recv, device):
        return pltpu.make_async_remote_copy(
            src_ref=src, dst_ref=dst, send_sem=self.sems.at[recv], recv_sem=self.sems.at[4 + recv],
            device_id=device, device_id_type=MESH,
        )

    def across(self):
        lat, lon = self.pos[:2]
        east, west = east_west(lon)
        left, right = self.targets["sides"]
        return [self.copy(self.sides[1], left, 0, (lat, east)), self.copy(self.sides[0], right, 1, (lat, west))]

    def along(self, step):
        lat, lon = self.pos[:2]
        east, west = east_west(lon)
        which, to = (1, 0) if step == 1 else (0, 1)
        row, first, last, _ = self.targets["rows"][to]
        return [
            self.copy(self.ends[which][1], first, 2 + to, (lat + step, east)),
            self.copy(self.ends[which][0], last, 2 + to, (lat + step, west)),
            self.copy(self.rows[which], row, 2 + to, (lat + step, lon)),
        ]

    def whole(self, step):
        to = 0 if step == 1 else 1
        row = self.targets["rows"][to][3]
        return self.copy(row, row, 2 + to, self.pos[:2])

    def start(self):
        for step in (1, -1):

            @pl.when(inside(self.pos[0], step))
            def _():
                for c in self.along(step):
                    c.start()

        for c in self.across():
            c.start()

    def arrive(self):
        for c in self.across():
            c.wait_recv()
        for step in (1, -1):

            @pl.when(inside(self.pos[0], -step))
            def _():
                self.whole(step).wait_recv()

    def drain(self):
        for c in self.across():
            c.wait_send()
        for step in (1, -1):

            @pl.when(inside(self.pos[0], step))
            def _():
                self.whole(step).wait_send()


def corner(stencil_ref, batch, o):
    s = stencil_ref[batch, 0, o]
    r = s // (COLS + 2)
    return r, s - r * (COLS + 2)


def main_kernel(
    cells, ens, observed_in, precision_in, weight_in, stencil_in, owned_in, pattern_in,
    gram_ref, proj_ref, tt_ref,
    observed, precision, weight, stencil, owned, pattern,
    tile, rim, edge, strip, edge_out, strip_out, prior, held,
    seen0, seenv0, seen1, seenv1, mark, markv,
    small_sem, local_sem, halo0_sem, halo1_sem, sem0, sem1,
):
    pos = position()
    lat, lon, x, y = pos
    smalls = [
        pltpu.make_async_copy(src, dst, small_sem.at[i])
        for i, (src, dst) in enumerate(
            (
                (observed_in, observed),
                (precision_in, precision),
                (weight_in, weight),
                (stencil_in, stencil),
                (owned_in, owned),
                (pattern_in, pattern),
            )
        )
    ]
    inner = pltpu.make_async_copy(cells, tile.at[pl.ds(1, ROWS), pl.ds(1, COLS)], local_sem.at[0])
    edges = [
        pltpu.make_async_copy(ens.at[0], edge.at[0], local_sem.at[1]),
        pltpu.make_async_copy(ens.at[ROWS - 1], edge.at[1], local_sem.at[2]),
        pltpu.make_async_copy(cells.at[:, 0], strip.at[0], local_sem.at[3]),
        pltpu.make_async_copy(cells.at[:, COLS - 1], strip.at[1], local_sem.at[4]),
    ]
    for c in smalls + [inner] + edges:
        c.start()
    first = Exchange(pos, seen0, seenv0, sem0)
    second = Exchange(pos, seen1, seenv1, sem1)
    first.blank()
    second.blank()
    rim[BLANK] = jnp.zeros((1, N), F32)
    for step, r, to in ((-1, 0, TOP), (1, ROWS + 1, BOTTOM)):

        @pl.when(jnp.logical_not(inside(lat, step)))
        def _():
            tile[r] = jnp.zeros((COLS + 2, 1, N), F32)
            rim[pl.ds(to, COLS + 2)] = jnp.zeros((COLS + 2, 1, N), F32)

    enter(pos)

    halo = Halo(
        pos,
        halo0_sem,
        rows=(cells.at[0], cells.at[ROWS - 1]),
        ends=((cells.at[0, 0], cells.at[0, COLS - 1]), (cells.at[ROWS - 1, 0], cells.at[ROWS - 1, COLS - 1])),
        sides=(cells.at[:, 0], cells.at[:, COLS - 1]),
        targets={
            "sides": (tile.at[pl.ds(1, ROWS), 0], tile.at[pl.ds(1, ROWS), COLS + 1]),
            "rows": tuple(
                (tile.at[r, pl.ds(1, COLS)], tile.at[r, 0], tile.at[r, COLS + 1], tile.at[r]) for r in (0, ROWS + 1)
            ),
        },
    )
    halo.start()
    for c in smalls:
        c.wait()
    masks(pos, 0, pattern, mark.at[0], markv.at[0])
    inner.wait()
    halo.arrive()

    for o in range(SLOTS):
        r, c = corner(stencil, 0, o)
        total = jnp.zeros((1, N), F32)
        for k in range(4):
            total = total + weight[0, k, o] * tile[r + k // 2, c + k % 2]
        prior[pl.ds(o, 1), :] = total
    first.start(*observe(0, prior[...], observed, precision, owned))
    for o in range(SLOTS):
        r, c = corner(stencil, 1, o)
        total = jnp.zeros((1, N), F32)
        for k in range(4):
            rk, ck = r + k // 2, c + k % 2
            own = (rk >= 1) & (rk <= ROWS) & (ck >= 1) & (ck <= COLS)
            total = total + jnp.where(own, weight[1, k, o], 0.0) * tile[rk, ck]
        held[pl.ds(o, 1), :] = total
    masks(pos, 1, pattern, mark.at[1], markv.at[1])
    for c in edges:
        c.wait()
    gram, proj = first.finish(mark.at[0], markv.at[0])

    tt = transform_t(gram, proj)
    for i in range(2):
        edge_out[i] = times(edge[i], tt).reshape(COLS, 1, N)
        strip_out[i] = times(strip[i].reshape(ROWS, N), tt).reshape(ROWS, 1, N)
    halo2 = Halo(
        pos,
        halo1_sem,
        rows=(edge_out.at[0], edge_out.at[1]),
        ends=tuple((edge_out.at[i, pl.ds(0, 1)], edge_out.at[i, pl.ds(COLS - 1, 1)]) for i in range(2)),
        sides=(strip_out.at[0], strip_out.at[1]),
        targets={
            "sides": (rim.at[pl.ds(LEFT, ROWS)], rim.at[pl.ds(RIGHT, ROWS)]),
            "rows": tuple(
                (
                    rim.at[pl.ds(to + 1, COLS)],
                    rim.at[pl.ds(to, 1)],
                    rim.at[pl.ds(to + COLS + 1, 1)],
                    rim.at[pl.ds(to, COLS + 2)],
                )
                for to in (TOP, BOTTOM)
            ),
        },
    )
    halo2.start()
    tt_ref[...] = tt
    prior[...] = times(held[...], tt)
    halo2.arrive()
    for o in range(SLOTS):
        r, c = corner(stencil, 1, o)
        total = prior[pl.ds(o, 1), :]
        for k in range(4):
            rk, ck = r + k // 2, c + k % 2
            where = jnp.where(ck == 0, LEFT - 1 + rk, jnp.where(ck == COLS + 1, RIGHT - 1 + rk, BLANK))
            where = jnp.where(rk == 0, TOP + ck, jnp.where(rk == ROWS + 1, BOTTOM + ck, where))
            total = total + weight[1, k, o] * rim[where]
        prior[pl.ds(o, 1), :] = total
    second.start(*observe(1, prior[...], observed, precision, owned))
    gram_ref[...], proj_ref[...] = second.finish(mark.at[1], markv.at[1])
    halo.drain()
    first.drain()
    halo2.drain()
    second.drain()


CHUNK = 512


def last_kernel(gram, proj, tt_ref, ens, out, cells, moved, in_sem, out_sem):
    chunks = ROWS * COLS // CHUNK
    loads = [
        pltpu.make_async_copy(ens.at[pl.ds(i * CHUNK, CHUNK)], cells.at[pl.ds(i * CHUNK, CHUNK)], in_sem.at[i])
        for i in range(chunks)
    ]
    for c in loads:
        c.start()
    tt = transform_t(gram[...], proj[...])
    both = jnp.dot(tt, tt_ref[...], precision=lax.Precision.HIGHEST, preferred_element_type=F32)
    high = both.astype(BF16)
    low = (both - high.astype(F32)).astype(BF16)
    right = jnp.concatenate(
        [jnp.concatenate([high, high], axis=1), jnp.concatenate([low, jnp.zeros_like(low)], axis=1)], axis=0
    )
    stores = []
    for i in range(chunks):
        rows = pl.ds(i * CHUNK, CHUNK)
        loads[i].wait()
        xs = cells[rows, :]
        xh = xs.astype(BF16)
        xl = (xs - xh.astype(F32)).astype(BF16)
        res = lax.dot_general(
            jnp.concatenate([xh, xl], axis=1), right, (((1,), (1,)), ((), ())), preferred_element_type=F32
        )
        moved[rows, :] = res[:, :N] + res[:, N:]
        c = pltpu.make_async_copy(moved.at[rows], out.at[rows], out_sem.at[i])
        c.start()
        stores.append(c)
    for c in stores:
        c.wait()


def shape(*dims):
    return jax.ShapeDtypeStruct(dims, F32)


VM = pl.BlockSpec(memory_space=pltpu.VMEM)
HBM = pl.BlockSpec(memory_space=pltpu.HBM)


def local(ensemble, observed, precision, interp_weight, stencil, owned, pattern):
    cells = ensemble.reshape(ROWS, COLS, 1, N)
    small = (
        observed.reshape(2, 1, SLOTS),
        precision.reshape(2, 1, SLOTS),
        interp_weight.reshape(2, 4, SLOTS),
        stencil.reshape(2, 4, SLOTS),
        owned.reshape(2, 1, SLOTS),
        pattern.transpose(0, 1, 3, 2, 4).reshape(2, 5, 1, LONS),
    )
    blocks = [pltpu.VMEM((5, LONS, SLOTS, N), BF16), pltpu.VMEM((5, LONS, 1, N), F32)]
    gram, proj, tt = pl.pallas_call(
        main_kernel,
        out_shape=(shape(N, N), shape(1, N), shape(N, N)),
        in_specs=[HBM] * 8,
        out_specs=(VM, VM, VM),
        scratch_shapes=[pltpu.SMEM(a.shape, a.dtype) for a in small]
        + [
            pltpu.VMEM((ROWS + 2, COLS + 2, 1, N), F32),
            pltpu.VMEM((RIM, 1, N), F32),
            pltpu.VMEM((2, COLS, N), F32),
            pltpu.VMEM((2, ROWS, 1, N), F32),
            pltpu.VMEM((2, COLS, 1, N), F32),
            pltpu.VMEM((2, ROWS, 1, N), F32),
            pltpu.VMEM((SLOTS, N), F32),
            pltpu.VMEM((SLOTS, N), F32),
        ]
        + blocks
        + blocks
        + [pltpu.VMEM((2, 5, LONS, SLOTS, N), BF16), pltpu.VMEM((2, 5, LONS, 1, N), F32)]
        + [pltpu.SemaphoreType.DMA((len(small),)), pltpu.SemaphoreType.DMA((5,))]
        + [pltpu.SemaphoreType.DMA((8,))] * 2
        + [pltpu.SemaphoreType.DMA((2, 1 + len(GROUPS) + 2 * len(NEAR)))] * 2,
        compiler_params=pltpu.CompilerParams(collective_id=0, has_side_effects=True, vmem_limit_bytes=VMEM_BYTES),
        name="main",
    )(*(pltpu.with_memory_space_constraint(a, pltpu.HBM) for a in (cells, ensemble) + small))
    chunks = ROWS * COLS // CHUNK
    out = pl.pallas_call(
        last_kernel,
        out_shape=shape(ROWS * COLS, N),
        in_specs=[VM, VM, VM, HBM],
        out_specs=HBM,
        scratch_shapes=[
            pltpu.VMEM((ROWS * COLS, N), F32),
            pltpu.VMEM((ROWS * COLS, N), F32),
            pltpu.SemaphoreType.DMA((chunks,)),
            pltpu.SemaphoreType.DMA((chunks,)),
        ],
        compiler_params=pltpu.CompilerParams(vmem_limit_bytes=VMEM_BYTES),
        name="last",
    )(gram, proj, tt, pltpu.with_memory_space_constraint(ensemble.reshape(ROWS * COLS, N), pltpu.HBM))
    return out.reshape(ROWS, COLS, N)


def solution(mesh):
    placed = (
        P("lat", "lon", None),
        P(None, "lat", "lon", None),
        P(None, "lat", "lon", None),
        P(None, "lat", "lon", None, None),
        P(None, "lat", "lon", None, None),
        P(None, "lat", "lon", None),
        P(None, "lat", "lon", None, None),
    )
    return jax.shard_map(
        local, mesh=mesh, in_specs=placed, out_specs=P("lat", "lon", None), check_vma=False
    )
```

time: 72.6 us -> 56.2 us (0.77)
  Pallas kernels: 66.5 us -> 55.7 us
  local copies, waits for them, and re-layouts: 5.71 us -> 0 us
    pallas_call x3 -> x1, Pallas kernels: 59.2 us -> 47.9 us  [local(): pl.pallas_call(main_kernel, out_shape=(shape(N, N), shape(1, N), shape(N,...]
    unnamed x17 -> x0, local copies, waits for them, and re-layouts: 5.7 us -> none
where the time goes in v2:
time: 56.2 us; the launch traced here: 55.7 us
  Pallas kernels  55.7 us (99%)
    pallas_call x1, Pallas kernels, local(): pl.pallas_call(main_kernel, out_shape=(shape(N, N), shape(1, N), shape(N,...  47.9 us
    pallas_call x1, Pallas kernels, local(): pl.pallas_call(last_kernel, out_shape=shape(ROWS * COLS, N), in_specs=[VM...  7.75 us

profile of v2, /device:TPU:1, one launch (start us, length us, event | category | flops | bytes accessed | tf_op | source)
XLA Modules:
  0.0 55.7 jit_solution(10013622720137351181)
XLA Ops:
  0.0 47.9 %main.1 = (f32[128,128]{1,0:T(8,128)S(1)}, f32[1,128]{1,0:T(1,128)S(1)}, f32[128,128]{1,0:T(8,128)S(1)}) custom-call(f32[32,128,1,128]{3,2,1,0:T(1,128)} %bitcast.15, f32[32,128,128]{2,1,0:T(8,128)} %ens.1, f32[2,1,8]{2,1,0:T(1,128)} %bitcast.20, f32[2,1,8]{2,1,0:T(1,128)} %bitcast.21, f32[2,4,8]{2,1,0:T(4,128)} %bitcast.18, s32[2,4,8]{2,1,0:T(4,128)} %bitcast.19, ...), custom_call_target="tpu_custom_call" | custom-call | tf_op jit(solution)/shard_map/main/pallas_call | solution.py:527
  47.9 7.8 %last.1 = f32[4096,128]{1,0:T(8,128)} custom-call(f32[128,128]{1,0:T(8,128)S(1)} %get-tuple-element.8.gram, f32[1,128]{1,0:T(1,128)S(1)} %get-tuple-element.9.proj, f32[128,128]{1,0:T(8,128)S(1)} %get-tuple-element.10.tt_ref, f32[4096,128]{1,0:T(8,128)} %bitcast.16), custom_call_target="tpu_custom_call" | custom-call | tf_op jit(solution)/shard_map/last/pallas_call | solution.py:553

commit v3 on v2

v3 whole, which is shorter than its diff:
```python
import functools
import math
import jax
import jax.numpy as jnp
from jax import lax
from jax.experimental import pallas as pl
from jax.experimental.pallas import tpu as pltpu
from jax.sharding import PartitionSpec as P

MESH = pl.DeviceIdType.MESH
F32 = jnp.float32
BF16 = jnp.bfloat16
ROWS, COLS, N = 32, 128, 128
SLOTS = 8
LATS, LONS = 24, 32
YS, XS = 8, 4
AROUND = ((-1, -1), (-1, 0), (-1, 1), (0, -1), (0, 1), (1, -1), (1, 0), (1, 1))
THIRDS = ((0, 3, -1), (3, 5, 0), (5, 8, 1))
NB = N // 8
NEAR = (-2, -1, 1, 2)
OWN = len(NEAR)
SLOT = sorted(
    ((dx, dy) for dx in (-1, 0, 1, 2) for dy in (-3, -2, -1, 0, 1, 2, 3, 4)), key=lambda p: (abs(p[0]) + abs(p[1]), p)
)
HOPS = [abs(dx) + abs(dy) for dx, dy in SLOT]
CUTS = (0, sum(h <= 2 for h in HOPS), sum(h <= 3 for h in HOPS), sum(h <= 4 for h in HOPS), LONS)
GROUPS = tuple(zip(CUTS[:-1], CUTS[1:]))
PAIRS = SLOTS // 2 + 1
VMEM_BYTES = 48 * 2**20


def split3(x):
    high = x.astype(BF16).astype(F32)
    rest = x - high
    mid = rest.astype(BF16).astype(F32)
    return high, mid, rest - mid


def outer8(r, g):
    rh, rm, rl = split3(r)
    gh, gm, gl = split3(g)
    lhs = jnp.concatenate([rh, rh, rm, rh, rl, rm], axis=0).astype(BF16)
    rhs = jnp.concatenate([gh, gm, gh, gl, gh, gm], axis=0).astype(BF16)
    return lax.dot_general(lhs, rhs, (((0,), (0,)), ((), ())), preferred_element_type=F32)


def spread_row(x, k):
    return jnp.broadcast_to(x[k : k + 1, :], (8, N))


def spread_col(x, c):
    return jnp.broadcast_to(x[:, c : c + 1], (8, N))


def transform_t(gram, proj):
    lane = lax.broadcasted_iota(jnp.int32, (8, N), 1)
    sub = lax.broadcasted_iota(jnp.int32, (8, N), 0)
    prow = jnp.broadcast_to(proj, (8, N))
    w = [gram[8 * i : 8 * i + 8, :] + jnp.where(lane == sub + 8 * i, N - 1.0, 0.0) for i in range(NB)]
    inverse, sums = [], []
    acc = jnp.zeros((8, N), F32)
    for j in range(NB):
        c0 = 8 * j
        wj = w[j]
        cols = [spread_col(wj, c0 + k) for k in range(8)]
        here = (lane >= c0) & (lane < c0 + 8)
        f = jnp.where(here, jnp.where(lane == sub + c0, 1.0, 0.0), wj)
        for k in range(8):
            d = spread_row(cols[k], k)
            below = jnp.where(sub == k, 0.0, cols[k])
            inv = 1.0 / d
            if k:
                lower = jnp.where(sub == k, f, lower)
                diag = jnp.where(sub == k, d, diag)
                inverse_diag = jnp.where(sub == k, inv, inverse_diag)
            else:
                lower, diag, inverse_diag = f, d, inv
            for t in range(k + 1, 8):
                cols[t] = cols[t] - (below * spread_row(cols[t], k)) * inv
            f = f - (below * spread_row(f, k)) * inv
        g = f * inverse_diag
        lj = jnp.where(lane <= c0 + 7, lower * lax.rsqrt(diag), 0.0)
        inverse.append(lj)
        sums.append(jnp.sum(lj, axis=1, keepdims=True))
        acc = acc + lj * jnp.sum(lj * prow, axis=1, keepdims=True)
        if j < NB - 1:
            nxt = w[j + 1]
            terms = [spread_col(nxt, c0 + k) * spread_row(g, k) for k in range(8)]
            while len(terms) > 1:
                terms = [a + b for a, b in zip(terms[::2], terms[1::2])]
            upd = jnp.where(here, 0.0, nxt) - terms[0]
            if j < NB - 2:
                p = outer8(wj, g)
                for i in range(j + 2, NB):
                    w[i] = jnp.where(here, 0.0, w[i]) - p[8 * i : 8 * i + 8, :]
            w[j + 1] = upd
    weights = jnp.sum(acc, axis=0, keepdims=True)
    total = jnp.sum(weights, axis=1, keepdims=True)
    root = math.sqrt(N - 1.0)
    out = []
    for i in range(NB):
        fix = (1.0 - (root * sums[i] + total)) * (1.0 / N)
        out.append(root * inverse[i] + weights + fix)
    return jnp.concatenate(out, axis=0)


def times(x, tt):
    return lax.dot_general(
        x, tt, (((1,), (1,)), ((), ())), precision=lax.Precision.HIGHEST, preferred_element_type=F32
    )


def position():
    lat, lon = lax.axis_index("lat"), lax.axis_index("lon")
    return lat, lon, lon // YS, lax.rem(lon, YS)


def inside(lat, step):
    return (lat + step >= 0) & (lat + step < LATS)


def east_west(lon):
    return lax.rem(lon + 1, LONS), lax.rem(lon + LONS - 1, LONS)


def lon_at(x, y, dx, dy):
    return lax.rem(x + dx + XS, XS) * YS + lax.rem(y + dy + YS, YS)


def announce(pos):
    lat, lon, x, y = pos
    barrier = pltpu.get_barrier_semaphore()

    def greet(a, c):
        pl.semaphore_signal(barrier, inc=1, device_id=(a, c), device_id_type=MESH)

    east, west = east_west(lon)
    for step in NEAR:

        @pl.when(inside(lat, step))
        def _():
            greet(lat + step, lon)
            if abs(step) == 1:
                greet(lat + step, east)
                greet(lat + step, west)

    greet(lat, east)
    greet(lat, west)
    for dx, dy in SLOT[:0:-1]:
        greet(lat, lon_at(x, y, -dx, -dy))


def enter(pos):
    lat = pos[0]
    count = LONS - 1 + 2
    for step in NEAR:
        count = count + jnp.where(inside(lat, step), 3 if abs(step) == 1 else 1, 0)
    pl.semaphore_wait(pltpu.get_barrier_semaphore(), count)


def masks(pos, batch, pattern_ref, mark, markv, pick):
    lat, lon, x, y = pos

    @pl.loop(0, OWN + 1)
    def _(d):
        line = jnp.where(d == OWN, 2, jnp.where(d < 2, d, d + 1))
        for i, (dx, dy) in enumerate(SLOT):
            value = pattern_ref[batch, line, 0, lon_at(x, y, dx, dy)].astype(F32)
            both = jnp.full((PAIRS - 1, 2, N), value, F32).astype(BF16)
            mark[d, i, pl.ds(0, PAIRS - 1)] = both
            mark[d, i, PAIRS - 1] = jnp.zeros((2, N), BF16)
            markv[d, i, pl.ds(0, PAIRS - 1)] = jnp.zeros((PAIRS - 1, 2, N), BF16)
            markv[d, i, PAIRS - 1] = both[0]

    first = (lax.broadcasted_iota(jnp.int32, (16, N), 1) == 0).astype(F32).astype(BF16)
    for d in range(OWN + 1):
        pick[d] = lax.dot_general(
            first, markv[d].reshape(LONS * PAIRS * 2, N), (((1,), (1,)), ((), ())), preferred_element_type=F32
        ).astype(BF16)


def observe(batch, prior, observed_ref, precision_ref, owned_ref):
    sub = lax.broadcasted_iota(jnp.int32, (SLOTS, N), 0)
    obs = jnp.zeros((SLOTS, N), F32)
    prec = jnp.zeros((SLOTS, N), F32)
    own = jnp.zeros((SLOTS, N), F32)
    for o in range(SLOTS):
        obs = jnp.where(sub == o, observed_ref[batch, 0, o], obs)
        prec = jnp.where(sub == o, precision_ref[batch, 0, o], prec)
        own = jnp.where(sub == o, owned_ref[batch, 0, o].astype(F32), own)
    root = jnp.sqrt(prec) * own
    mean = jnp.sum(prior, axis=1, keepdims=True) * (1.0 / N)
    scaled = (root * (prior - mean)).astype(BF16)
    innov = (root * (obs - mean)).astype(BF16)
    vector = jnp.sum(scaled.astype(F32) * innov.astype(F32), axis=0, keepdims=True)
    return scaled, vector


class Exchange:
    def __init__(self, pos, seen, sems):
        self.pos, self.seen, self.sems = pos, seen, sems

    def copy(self, src, size, dst, device, send, recv):
        (sd, si), (dd, di) = src, dst
        return pltpu.make_async_remote_copy(
            src_ref=self.seen.at[sd, pl.ds(si, size)], dst_ref=self.seen.at[dd, pl.ds(di, size)],
            send_sem=self.sems.at[send], recv_sem=self.sems.at[recv], device_id=device, device_id_type=MESH,
        )

    def blank(self):
        for step in NEAR:

            @pl.when(jnp.logical_not(inside(self.pos[0], step)))
            def _():
                self.seen[NEAR.index(step)] = jnp.zeros(self.seen.shape[1:], BF16)

    def row(self, i, g):
        lat, _, x, y = self.pos
        dx, dy = SLOT[i]
        return self.copy((OWN, 0), 1, (OWN, i), (lat, lon_at(x, y, -dx, -dy)), 0, 1 + g)

    def row_group(self, g):
        start, stop = max(GROUPS[g][0], 1), GROUPS[g][1]
        return self.copy((OWN, start), stop - start, (OWN, start), self.pos[:2], 0, 1 + g)

    def relay(self, k, start, stop):
        lat, lon = self.pos[:2]
        send = 1 + len(GROUPS) + k
        return self.copy(
            (OWN, start), stop - start, (OWN - 1 - k, start), (lat + NEAR[k], lon), send, send + len(NEAR)
        )

    def start(self, scaled, vector):
        for i in range(PAIRS - 1):
            self.seen[OWN, 0, i] = scaled[2 * i : 2 * i + 2, :]
        high = vector.astype(BF16)
        self.seen[OWN, 0, PAIRS - 1] = jnp.concatenate([high.astype(F32), vector - high.astype(F32)], axis=0).astype(BF16)
        for g, (start, stop) in reversed(tuple(enumerate(GROUPS))):
            for i in reversed(range(max(start, 1), stop)):
                self.row(i, g).start()

    def finish(self, mark, pick):
        lat = self.pos[0]

        def term(d, size):
            flat = self.seen[pl.ds(d, size)].reshape(size * LONS * PAIRS * 2, N)
            marked = flat * mark[pl.ds(d, size)].reshape(size * LONS * PAIRS * 2, N)
            gram = lax.dot_general(marked, flat, (((0,), (0,)), ((), ())), preferred_element_type=F32)
            proj = jnp.zeros((16, N), F32)
            for i in range(size):
                rows = flat[i * LONS * PAIRS * 2 : (i + 1) * LONS * PAIRS * 2]
                proj = proj + jnp.dot(pick[d + i], rows, preferred_element_type=F32)
            return gram, proj[0:1]

        for g, (start, stop) in enumerate(GROUPS):
            self.row_group(g).wait_recv()
            for k, step in enumerate(NEAR):

                @pl.when(inside(lat, step))
                def _():
                    self.relay(k, start, stop).start()

        gram, proj = term(OWN, 1)
        for k, step in enumerate(NEAR):

            @pl.when(inside(lat, -step))
            def _():
                self.relay(k, 0, LONS).wait_recv()

        more, morev = term(0, OWN)
        return gram + more, proj + morev

    def drain(self):
        self.copy((OWN, 1), LONS - 1, (OWN, 1), self.pos[:2], 0, 1).wait_send()
        for k, step in enumerate(NEAR):

            @pl.when(inside(self.pos[0], step))
            def _():
                self.relay(k, 0, LONS).wait_send()


class Around:
    def __init__(self, pos, src, dst, sems):
        self.pos, self.src, self.dst, self.sems = pos, src, dst, sems

    def copies(self, g):
        lat, lon = self.pos[:2]
        start, stop, step = THIRDS[g]
        return [
            pltpu.make_async_remote_copy(
                src_ref=self.src.at[n], dst_ref=self.dst.at[7 - n],
                send_sem=self.sems.at[g], recv_sem=self.sems.at[5 - g],
                device_id=(lat + step, lax.rem(lon + AROUND[n][1] + LONS, LONS)), device_id_type=MESH,
            )
            for n in range(start, stop)
        ]

    def group(self, g):
        start, stop, _ = THIRDS[g]
        return pltpu.make_async_remote_copy(
            src_ref=self.src.at[pl.ds(start, stop - start)], dst_ref=self.dst.at[pl.ds(start, stop - start)],
            send_sem=self.sems.at[g], recv_sem=self.sems.at[3 + g], device_id=self.pos[:2], device_id_type=MESH,
        )

    def each(self, act):
        for g, (_, _, step) in enumerate(THIRDS):
            if step == 0:
                act(g)
            else:
                pl.when(inside(self.pos[0], step))(functools.partial(act, g))

    def blank(self):
        for start, stop, step in THIRDS:

            @pl.when(jnp.logical_not(inside(self.pos[0], step)))
            def _():
                self.dst[pl.ds(start, stop - start)] = jnp.zeros((stop - start, SLOTS, N), F32)

    def start(self):
        def act(g):
            for c in self.copies(g):
                c.start()

        self.each(act)

    def arrive(self):
        self.each(lambda g: self.group(g).wait_recv())

    def drain(self):
        self.each(lambda g: self.group(g).wait_send())


class Halo:
    def __init__(self, pos, sems, rows, ends, sides, targets):
        self.pos, self.sems, self.rows, self.ends, self.sides, self.targets = pos, sems, rows, ends, sides, targets

    def copy(self, src, dst, recv, device):
        return pltpu.make_async_remote_copy(
            src_ref=src, dst_ref=dst, send_sem=self.sems.at[recv], recv_sem=self.sems.at[4 + recv],
            device_id=device, device_id_type=MESH,
        )

    def across(self):
        lat, lon = self.pos[:2]
        east, west = east_west(lon)
        left, right = self.targets["sides"]
        return [self.copy(self.sides[1], left, 0, (lat, east)), self.copy(self.sides[0], right, 1, (lat, west))]

    def along(self, step):
        lat, lon = self.pos[:2]
        east, west = east_west(lon)
        which, to = (1, 0) if step == 1 else (0, 1)
        row, first, last, _ = self.targets["rows"][to]
        return [
            self.copy(self.ends[which][1], first, 2 + to, (lat + step, east)),
            self.copy(self.ends[which][0], last, 2 + to, (lat + step, west)),
            self.copy(self.rows[which], row, 2 + to, (lat + step, lon)),
        ]

    def whole(self, step):
        to = 0 if step == 1 else 1
        row = self.targets["rows"][to][3]
        return self.copy(row, row, 2 + to, self.pos[:2])

    def start(self):
        for step in (1, -1):

            @pl.when(inside(self.pos[0], step))
            def _():
                for c in self.along(step):
                    c.start()

        for c in self.across():
            c.start()

    def arrive(self):
        for c in self.across():
            c.wait_recv()
        for step in (1, -1):

            @pl.when(inside(self.pos[0], -step))
            def _():
                self.whole(step).wait_recv()

    def drain(self):
        for c in self.across():
            c.wait_send()
        for step in (1, -1):

            @pl.when(inside(self.pos[0], step))
            def _():
                self.whole(step).wait_send()


def corner(stencil_ref, batch, o):
    s = stencil_ref[batch, 0, o]
    r = s // (COLS + 2)
    return r, s - r * (COLS + 2)


def main_kernel(
    cells, observed_in, precision_in, weight_in, stencil_in, owned_in, pattern_in,
    gram_ref, proj_ref, tt_ref,
    observed, precision, weight, stencil, owned, pattern,
    tile, prior, ask, asked, answer, answered, seen0, seen1, mark, markv, pick,
    small_sem, inner_sem, halo_sem, ask_sem, answer_sem, sem0, sem1,
):
    pos = position()
    lat = pos[0]
    announce(pos)
    inner = pltpu.make_async_copy(cells, tile.at[pl.ds(1, ROWS), pl.ds(1, COLS)], inner_sem)
    inner.start()
    smalls = [
        pltpu.make_async_copy(src, dst, small_sem.at[i])
        for i, (src, dst) in enumerate(
            (
                (pattern_in, pattern),
                (observed_in, observed),
                (precision_in, precision),
                (weight_in, weight),
                (stencil_in, stencil),
                (owned_in, owned),
            )
        )
    ]
    for c in smalls:
        c.start()
    first = Exchange(pos, seen0, sem0)
    second = Exchange(pos, seen1, sem1)
    asks = Around(pos, ask.at[pl.ds(0, 8)], asked, ask_sem)
    answers = Around(pos, answer, answered, answer_sem)
    for part in (first, second, asks, answers):
        part.blank()
    for step, r in ((-1, 0), (1, ROWS + 1)):

        @pl.when(jnp.logical_not(inside(lat, step)))
        def _():
            tile[r] = jnp.zeros((COLS + 2, 1, N), F32)

    halo = Halo(
        pos,
        halo_sem,
        rows=(tile.at[1, pl.ds(1, COLS)], tile.at[ROWS, pl.ds(1, COLS)]),
        ends=((tile.at[1, 1], tile.at[1, COLS]), (tile.at[ROWS, 1], tile.at[ROWS, COLS])),
        sides=(tile.at[pl.ds(1, ROWS), 1], tile.at[pl.ds(1, ROWS), COLS]),
        targets={
            "sides": (tile.at[pl.ds(1, ROWS), 0], tile.at[pl.ds(1, ROWS), COLS + 1]),
            "rows": tuple(
                (tile.at[r, pl.ds(1, COLS)], tile.at[r, 0], tile.at[r, COLS + 1], tile.at[r]) for r in (0, ROWS + 1)
            ),
        },
    )
    inner.wait()
    enter(pos)
    halo.start()
    for c in smalls:
        c.wait()
    masks(pos, 0, pattern, mark.at[0], markv, pick.at[0])
    halo.arrive()

    for o in range(SLOTS):
        r, c = corner(stencil, 0, o)
        total = jnp.zeros((1, N), F32)
        for k in range(4):
            total = total + weight[0, k, o] * tile[r + k // 2, c + k % 2]
        prior[pl.ds(o, 1), :] = total
    first.start(*observe(0, prior[...], observed, precision, owned))

    for o in range(SLOTS):
        r, c = corner(stencil, 1, o)
        shares = [jnp.zeros((1, N), F32) for _ in range(9)]
        for k in range(4):
            rk, ck = r + k // 2, c + k % 2
            up, down = rk == 0, rk == ROWS + 1
            left, right = ck == 0, ck == COLS + 1
            middle, centre = jnp.logical_not(up | down), jnp.logical_not(left | right)
            cell, scale = tile[rk, ck], weight[1, k, o]
            for n, (dr, dc) in enumerate(AROUND + ((0, 0),)):
                there = (up, middle, down)[dr + 1] & (left, centre, right)[dc + 1]
                shares[n] = shares[n] + jnp.where(there, scale, 0.0) * cell
        for n in range(9):
            ask[n, pl.ds(o, 1), :] = shares[n]
    asks.start()
    masks(pos, 1, pattern, mark.at[1], markv, pick.at[1])
    gram, proj = first.finish(mark.at[0], pick.at[0])
    asks.arrive()

    tt = transform_t(gram, proj)
    answer[...] = times(asked[...].reshape(8 * SLOTS, N), tt).reshape(8, SLOTS, N)
    answers.start()
    tt_ref[...] = tt
    total = times(ask[8], tt)
    answers.arrive()
    for n in range(8):
        total = total + answered[n]
    second.start(*observe(1, total, observed, precision, owned))
    gram_ref[...], proj_ref[...] = second.finish(mark.at[1], pick.at[1])
    for part in (halo, first, asks, answers, second):
        part.drain()


CHUNK = 1024


def last_kernel(gram, proj, tt_ref, ens, out, cells, moved, in_sem, out_sem):
    chunks = ROWS * COLS // CHUNK
    load = pltpu.make_async_copy(ens, cells, in_sem)
    load.start()
    tt = transform_t(gram[...], proj[...])
    both = jnp.dot(tt, tt_ref[...], precision=lax.Precision.HIGHEST, preferred_element_type=F32)
    high = both.astype(BF16)
    low = (both - high.astype(F32)).astype(BF16)
    right = jnp.concatenate(
        [jnp.concatenate([high, high], axis=1), jnp.concatenate([low, jnp.zeros_like(low)], axis=1)], axis=0
    )
    stores = []
    load.wait()
    for i in range(chunks):
        rows = pl.ds(i * CHUNK, CHUNK)
        xs = cells[rows, :]
        xh = xs.astype(BF16)
        xl = (xs - xh.astype(F32)).astype(BF16)
        res = lax.dot_general(
            jnp.concatenate([xh, xl], axis=1), right, (((1,), (1,)), ((), ())), preferred_element_type=F32
        )
        moved[rows, :] = res[:, :N] + res[:, N:]
        c = pltpu.make_async_copy(moved.at[rows], out.at[rows], out_sem.at[i])
        c.start()
        stores.append(c)
    for c in stores:
        c.wait()


def shape(*dims):
    return jax.ShapeDtypeStruct(dims, F32)


VM = pl.BlockSpec(memory_space=pltpu.VMEM)
HBM = pl.BlockSpec(memory_space=pltpu.HBM)


def local(ensemble, observed, precision, interp_weight, stencil, owned, pattern):
    cells = ensemble.reshape(ROWS, COLS, 1, N)
    small = (
        observed.reshape(2, 1, SLOTS),
        precision.reshape(2, 1, SLOTS),
        interp_weight.reshape(2, 4, SLOTS),
        stencil.reshape(2, 4, SLOTS),
        owned.reshape(2, 1, SLOTS),
        pattern.transpose(0, 1, 3, 2, 4).reshape(2, 5, 1, LONS),
    )
    gram, proj, tt = pl.pallas_call(
        main_kernel,
        out_shape=(shape(N, N), shape(1, N), shape(N, N)),
        in_specs=[HBM] * 7,
        out_specs=(VM, VM, VM),
        scratch_shapes=[pltpu.SMEM(a.shape, a.dtype) for a in small]
        + [
            pltpu.VMEM((ROWS + 2, COLS + 2, 1, N), F32),
            pltpu.VMEM((SLOTS, N), F32),
            pltpu.VMEM((9, SLOTS, N), F32),
            pltpu.VMEM((8, SLOTS, N), F32),
            pltpu.VMEM((8, SLOTS, N), F32),
            pltpu.VMEM((8, SLOTS, N), F32),
            pltpu.VMEM((5, LONS, PAIRS, 2, N), BF16),
            pltpu.VMEM((5, LONS, PAIRS, 2, N), BF16),
            pltpu.VMEM((2, 5, LONS, PAIRS, 2, N), BF16),
            pltpu.VMEM((5, LONS, PAIRS, 2, N), BF16),
            pltpu.VMEM((2, 5, 16, LONS * PAIRS * 2), BF16),
            pltpu.SemaphoreType.DMA((len(small),)),
            pltpu.SemaphoreType.DMA,
            pltpu.SemaphoreType.DMA((8,)),
            pltpu.SemaphoreType.DMA((6,)),
            pltpu.SemaphoreType.DMA((6,)),
        ]
        + [pltpu.SemaphoreType.DMA((1 + len(GROUPS) + 2 * len(NEAR),))] * 2,
        compiler_params=pltpu.CompilerParams(collective_id=0, has_side_effects=True, vmem_limit_bytes=VMEM_BYTES),
        name="main",
    )(*(pltpu.with_memory_space_constraint(a, pltpu.HBM) for a in (cells,) + small))
    chunks = ROWS * COLS // CHUNK
    out = pl.pallas_call(
        last_kernel,
        out_shape=shape(ROWS * COLS, N),
        in_specs=[VM, VM, VM, HBM],
        out_specs=HBM,
        scratch_shapes=[
            pltpu.VMEM((ROWS * COLS, N), F32),
            pltpu.VMEM((ROWS * COLS, N), F32),
            pltpu.SemaphoreType.DMA,
            pltpu.SemaphoreType.DMA((chunks,)),
        ],
        compiler_params=pltpu.CompilerParams(vmem_limit_bytes=VMEM_BYTES),
        name="last",
    )(gram, proj, tt, pltpu.with_memory_space_constraint(ensemble.reshape(ROWS * COLS, N), pltpu.HBM))
    return out.reshape(ROWS, COLS, N)


def solution(mesh):
    placed = (
        P("lat", "lon", None),
        P(None, "lat", "lon", None),
        P(None, "lat", "lon", None),
        P(None, "lat", "lon", None, None),
        P(None, "lat", "lon", None, None),
        P(None, "lat", "lon", None),
        P(None, "lat", "lon", None, None),
    )
    return jax.shard_map(
        local, mesh=mesh, in_specs=placed, out_specs=P("lat", "lon", None), check_vma=False
    )
```

time: 56.2 us -> 54 us (0.961)
  Pallas kernels: 55.7 us -> 53.2 us
    pallas_call x1, Pallas kernels: 47.9 us -> 46.5 us  [local(): pl.pallas_call(main_kernel, out_shape=(shape(N, N), shape(1, N), shape(N,...]
    pallas_call x1, Pallas kernels: 7.75 us -> 6.69 us  [local(): pl.pallas_call(last_kernel, out_shape=shape(ROWS * COLS, N), in_specs=[VM...]
where the time goes in v3:
time: 54 us; the launch traced here: 53.2 us
  Pallas kernels  53.2 us (99%)
    pallas_call x1, Pallas kernels, local(): pl.pallas_call(main_kernel, out_shape=(shape(N, N), shape(1, N), shape(N,...  46.5 us
    pallas_call x1, Pallas kernels, local(): pl.pallas_call(last_kernel, out_shape=shape(ROWS * COLS, N), in_specs=[VM...  6.69 us

profile of v3, /device:TPU:1, one launch (start us, length us, event | category | flops | bytes accessed | tf_op | source)
XLA Modules:
  0.0 53.2 jit_solution(4324837695966447483)
XLA Ops:
  0.0 46.5 %main.1 = (f32[128,128]{1,0:T(8,128)S(1)}, f32[1,128]{1,0:T(1,128)S(1)}, f32[128,128]{1,0:T(8,128)S(1)}) custom-call(f32[32,128,1,128]{3,2,1,0:T(1,128)} %bitcast.15, f32[2,1,8]{2,1,0:T(1,128)} %bitcast.20, f32[2,1,8]{2,1,0:T(1,128)} %bitcast.21, f32[2,4,8]{2,1,0:T(4,128)} %bitcast.18, s32[2,4,8]{2,1,0:T(4,128)} %bitcast.19, s32[2,1,8]{2,1,0:T(1,128)} %bitcast.22, ...), custom_call_target="tpu_custom_call" | custom-call | tf_op jit(solution)/shard_map/main/pallas_call | solution.py:552
  46.5 6.7 %last.1 = f32[4096,128]{1,0:T(8,128)} custom-call(f32[128,128]{1,0:T(8,128)S(1)} %get-tuple-element.8.gram, f32[1,128]{1,0:T(1,128)S(1)} %get-tuple-element.9.proj, f32[128,128]{1,0:T(8,128)S(1)} %get-tuple-element.10.tt_ref, f32[4096,128]{1,0:T(8,128)} %bitcast.16), custom_call_target="tpu_custom_call" | custom-call | tf_op jit(solution)/shard_map/last/pallas_call | solution.py:581

commit v4 on v3

--- a/solution.py
+++ b/solution.py
@@ -146,16 +146,24 @@
 
     greet(lat, east)
     greet(lat, west)
-    for dx, dy in SLOT[:0:-1]:
-        greet(lat, lon_at(x, y, -dx, -dy))
+    for t in range(1, YS):
+        greet(lat, lon_at(x, y, 0, t))
+    for t in range(1, XS):
+        greet(lat, lon_at(x, y, t, 0))
 
 
 def enter(pos):
     lat = pos[0]
-    count = LONS - 1 + 2
+    count = YS - 1 + XS - 1 + 2
     for step in NEAR:
         count = count + jnp.where(inside(lat, step), 3 if abs(step) == 1 else 1, 0)
     pl.semaphore_wait(pltpu.get_barrier_semaphore(), count)
+
+
+def pass_on(pos, ready):
+    lat, _, x, y = pos
+    for t in range(1, YS):
+        pl.semaphore_signal(ready, inc=1, device_id=(lat, lon_at(x, y, 0, t)), device_id_type=MESH)
 
 
 def masks(pos, batch, pattern_ref, mark, markv, pick):
@@ -403,7 +411,7 @@
     gram_ref, proj_ref, tt_ref,
     observed, precision, weight, stencil, owned, pattern,
     tile, prior, ask, asked, answer, answered, seen0, seen1, mark, markv, pick,
-    small_sem, inner_sem, halo_sem, ask_sem, answer_sem, sem0, sem1,
+    small_sem, inner_sem, ready, halo_sem, ask_sem, answer_sem, sem0, sem1,
 ):
     pos = position()
     lat = pos[0]
@@ -453,6 +461,7 @@
     inner.wait()
     enter(pos)
     halo.start()
+    pass_on(pos, ready)
     for c in smalls:
         c.wait()
     masks(pos, 0, pattern, mark.at[0], markv, pick.at[0])
@@ -464,7 +473,9 @@
         for k in range(4):
             total = total + weight[0, k, o] * tile[r + k // 2, c + k % 2]
         prior[pl.ds(o, 1), :] = total
-    first.start(*observe(0, prior[...], observed, precision, owned))
+    scaled, vector = observe(0, prior[...], observed, precision, owned)
+    pl.semaphore_wait(ready, YS - 1)
+    first.start(scaled, vector)
 
     for o in range(SLOTS):
         r, c = corner(stencil, 1, o)
@@ -490,12 +501,14 @@
     answers.start()
     tt_ref[...] = tt
     total = times(ask[8], tt)
+    for part in (halo, first, asks):
+        part.drain()
     answers.arrive()
     for n in range(8):
         total = total + answered[n]
     second.start(*observe(1, total, observed, precision, owned))
     gram_ref[...], proj_ref[...] = second.finish(mark.at[1], pick.at[1])
-    for part in (halo, first, asks, answers, second):
+    for part in (answers, second):
         part.drain()
 
 
@@ -569,6 +582,7 @@
             pltpu.VMEM((2, 5, 16, LONS * PAIRS * 2), BF16),
             pltpu.SemaphoreType.DMA((len(small),)),
             pltpu.SemaphoreType.DMA,
+            pltpu.SemaphoreType.REGULAR,
             pltpu.SemaphoreType.DMA((8,)),
             pltpu.SemaphoreType.DMA((6,)),
             pltpu.SemaphoreType.DMA((6,)),

time: 54 us -> 52.7 us (0.976); the launches traced: 53.2 us -> 52.5 us
  Pallas kernels: 53.2 us -> 52.5 us
    pallas_call x1, Pallas kernels: 46.5 us -> 45.8 us  [local(): pl.pallas_call(main_kernel, out_shape=(shape(N, N), shape(1, N), shape(N,...]
where the time goes in v4:
time: 52.7 us; the launch traced here: 52.5 us
  Pallas kernels  52.5 us (100%)
    pallas_call x1, Pallas kernels, local(): pl.pallas_call(main_kernel, out_shape=(shape(N, N), shape(1, N), shape(N,...  45.8 us
    pallas_call x1, Pallas kernels, local(): pl.pallas_call(last_kernel, out_shape=shape(ROWS * COLS, N), in_specs=[VM...  6.69 us

profile of v4, /device:TPU:1, one launch (start us, length us, event | category | flops | bytes accessed | tf_op | source)
XLA Modules:
  0.0 52.5 jit_solution(451873574078833144)
XLA Ops:
  0.0 45.8 %main.1 = (f32[128,128]{1,0:T(8,128)S(1)}, f32[1,128]{1,0:T(1,128)S(1)}, f32[128,128]{1,0:T(8,128)S(1)}) custom-call(f32[32,128,1,128]{3,2,1,0:T(1,128)} %bitcast.15, f32[2,1,8]{2,1,0:T(1,128)} %bitcast.20, f32[2,1,8]{2,1,0:T(1,128)} %bitcast.21, f32[2,4,8]{2,1,0:T(4,128)} %bitcast.18, s32[2,4,8]{2,1,0:T(4,128)} %bitcast.19, s32[2,1,8]{2,1,0:T(1,128)} %bitcast.22, ...), custom_call_target="tpu_custom_call" | custom-call | tf_op jit(solution)/shard_map/main/pallas_call | solution.py:565
  45.8 6.7 %last.1 = f32[4096,128]{1,0:T(8,128)} custom-call(f32[128,128]{1,0:T(8,128)S(1)} %get-tuple-element.8.gram, f32[1,128]{1,0:T(1,128)S(1)} %get-tuple-element.9.proj, f32[128,128]{1,0:T(8,128)S(1)} %get-tuple-element.10.tt_ref, f32[4096,128]{1,0:T(8,128)} %bitcast.16), custom_call_target="tpu_custom_call" | custom-call | tf_op jit(solution)/shard_map/last/pallas_call | solution.py:595

commit v5 on v4

--- a/solution.py
+++ b/solution.py
@@ -16,7 +16,8 @@
 YS, XS = 8, 4
 AROUND = ((-1, -1), (-1, 0), (-1, 1), (0, -1), (0, 1), (1, -1), (1, 0), (1, 1))
 THIRDS = ((0, 3, -1), (3, 5, 0), (5, 8, 1))
-NB = N // 8
+DEEP = 16
+NB = N // DEEP
 NEAR = (-2, -1, 1, 2)
 OWN = len(NEAR)
 SLOT = sorted(
@@ -36,7 +37,7 @@
     return high, mid, rest - mid
 
 
-def outer8(r, g):
+def outer(r, g):
     rh, rm, rl = split3(r)
     gh, gm, gl = split3(g)
     lhs = jnp.concatenate([rh, rh, rm, rh, rl, rm], axis=0).astype(BF16)
@@ -45,27 +46,27 @@
 
 
 def spread_row(x, k):
-    return jnp.broadcast_to(x[k : k + 1, :], (8, N))
+    return jnp.broadcast_to(x[k : k + 1, :], (DEEP, N))
 
 
 def spread_col(x, c):
-    return jnp.broadcast_to(x[:, c : c + 1], (8, N))
+    return jnp.broadcast_to(x[:, c : c + 1], (DEEP, N))
 
 
 def transform_t(gram, proj):
-    lane = lax.broadcasted_iota(jnp.int32, (8, N), 1)
-    sub = lax.broadcasted_iota(jnp.int32, (8, N), 0)
-    prow = jnp.broadcast_to(proj, (8, N))
-    w = [gram[8 * i : 8 * i + 8, :] + jnp.where(lane == sub + 8 * i, N - 1.0, 0.0) for i in range(NB)]
+    lane = lax.broadcasted_iota(jnp.int32, (DEEP, N), 1)
+    sub = lax.broadcasted_iota(jnp.int32, (DEEP, N), 0)
+    prow = jnp.broadcast_to(proj, (DEEP, N))
+    w = [gram[DEEP * i : DEEP * i + DEEP, :] + jnp.where(lane == sub + DEEP * i, N - 1.0, 0.0) for i in range(NB)]
     inverse, sums = [], []
-    acc = jnp.zeros((8, N), F32)
+    acc = jnp.zeros((DEEP, N), F32)
     for j in range(NB):
-        c0 = 8 * j
+        c0 = DEEP * j
         wj = w[j]
-        cols = [spread_col(wj, c0 + k) for k in range(8)]
-        here = (lane >= c0) & (lane < c0 + 8)
+        cols = [spread_col(wj, c0 + k) for k in range(DEEP)]
+        here = (lane >= c0) & (lane < c0 + DEEP)
         f = jnp.where(here, jnp.where(lane == sub + c0, 1.0, 0.0), wj)
-        for k in range(8):
+        for k in range(DEEP):
             d = spread_row(cols[k], k)
             below = jnp.where(sub == k, 0.0, cols[k])
             inv = 1.0 / d
@@ -75,24 +76,24 @@
                 inverse_diag = jnp.where(sub == k, inv, inverse_diag)
             else:
                 lower, diag, inverse_diag = f, d, inv
-            for t in range(k + 1, 8):
+            for t in range(k + 1, DEEP):
                 cols[t] = cols[t] - (below * spread_row(cols[t], k)) * inv
             f = f - (below * spread_row(f, k)) * inv
         g = f * inverse_diag
-        lj = jnp.where(lane <= c0 + 7, lower * lax.rsqrt(diag), 0.0)
+        lj = jnp.where(lane <= c0 + DEEP - 1, lower * lax.rsqrt(diag), 0.0)
         inverse.append(lj)
         sums.append(jnp.sum(lj, axis=1, keepdims=True))
         acc = acc + lj * jnp.sum(lj * prow, axis=1, keepdims=True)
         if j < NB - 1:
             nxt = w[j + 1]
-            terms = [spread_col(nxt, c0 + k) * spread_row(g, k) for k in range(8)]
+            terms = [spread_col(nxt, c0 + k) * spread_row(g, k) for k in range(DEEP)]
             while len(terms) > 1:
                 terms = [a + b for a, b in zip(terms[::2], terms[1::2])]
             upd = jnp.where(here, 0.0, nxt) - terms[0]
             if j < NB - 2:
-                p = outer8(wj, g)
+                p = outer(wj, g)
                 for i in range(j + 2, NB):
-                    w[i] = jnp.where(here, 0.0, w[i]) - p[8 * i : 8 * i + 8, :]
+                    w[i] = jnp.where(here, 0.0, w[i]) - p[DEEP * i : DEEP * i + DEEP, :]
             w[j + 1] = upd
     weights = jnp.sum(acc, axis=0, keepdims=True)
     total = jnp.sum(weights, axis=1, keepdims=True)

time: 52.7 us -> 51.9 us (0.985)
  Pallas kernels: 52.5 us -> 51.7 us
where the time goes in v5:
time: 51.9 us; the launch traced here: 51.8 us
  Pallas kernels  51.7 us (100%)
    pallas_call x1, Pallas kernels, local(): pl.pallas_call(main_kernel, out_shape=(shape(N, N), shape(1, N), shape(N,...  45.4 us
    pallas_call x1, Pallas kernels, local(): pl.pallas_call(last_kernel, out_shape=shape(ROWS * COLS, N), in_specs=[VM...  6.33 us

profile of v5, /device:TPU:1, one launch (start us, length us, event | category | flops | bytes accessed | tf_op | source)
XLA Modules:
  0.0 51.8 jit_solution(15221282025218615679)
XLA Ops:
  0.0 45.4 %main.1 = (f32[128,128]{1,0:T(8,128)S(1)}, f32[1,128]{1,0:T(1,128)S(1)}, f32[128,128]{1,0:T(8,128)S(1)}) custom-call(f32[32,128,1,128]{3,2,1,0:T(1,128)} %bitcast.15, f32[2,1,8]{2,1,0:T(1,128)} %bitcast.20, f32[2,1,8]{2,1,0:T(1,128)} %bitcast.21, f32[2,4,8]{2,1,0:T(4,128)} %bitcast.18, s32[2,4,8]{2,1,0:T(4,128)} %bitcast.19, s32[2,1,8]{2,1,0:T(1,128)} %bitcast.22, ...), custom_call_target="tpu_custom_call" | custom-call | tf_op jit(solution)/shard_map/main/pallas_call | solution.py:566
  45.4 6.3 %last.1 = f32[4096,128]{1,0:T(8,128)} custom-call(f32[128,128]{1,0:T(8,128)S(1)} %get-tuple-element.8.gram, f32[1,128]{1,0:T(1,128)S(1)} %get-tuple-element.9.proj, f32[128,128]{1,0:T(8,128)S(1)} %get-tuple-element.10.tt_ref, f32[4096,128]{1,0:T(8,128)} %bitcast.16), custom_call_target="tpu_custom_call" | custom-call | tf_op jit(solution)/shard_map/last/pallas_call | solution.py:596
